TPU v7x, 256 devices: a whole 4x4x8 slice. The times are simulated.
256 devices in a mesh: ctx: 64 (over z_lo, x, y), rep: 4 (over z_hi, core).
Axes of the slice: x: 4, y: 4, z: 8 (z_hi: 2, z_lo: 4; z = z_hi * 4 + z_lo), core: 2. Of those that a mesh axis runs over, the one named last changes fastest.
Arguments:
- inputs: bfloat16 [4, 16384, 256], P('rep', 'ctx'), may hold values from -6 to 6
- w_expand: bfloat16 [512, 1024], replicated, may hold values from -0.25 to 0.25
- b_expand: float32 [1024], replicated, may hold values from -1 to 1
- w_reduce: bfloat16 [1024, 512], replicated, may hold values from -0.1875 to 0.1875
- b_reduce: float32 [512], replicated, may hold values from -0.5 to 0.5
- gate_logit: float32 [512], replicated, may hold values from -2 to 2
- cotangent: bfloat16 [4, 16384, 256], P('rep', 'ctx'), may hold values from -6 to 6
Outputs:
- outputs: bfloat16 [4, 16384, 256], P('rep', 'ctx')
- grad_inputs: bfloat16 [4, 16384, 256], P('rep', 'ctx')
- grad_w_expand: float32 [512, 1024], P('ctx')
- grad_b_expand: float32 [1024], replicated
- grad_w_reduce: float32 [1024, 512], P('ctx')
- grad_b_reduce: float32 [512], replicated
- grad_gate: float32 [512], replicated
All inputs are finite; a program needn't handle non-finite values.
Results may differ from a plain program's by a relative error of at most 0.018.
Values may be sent and summed in bfloat16 or wider, within the bound.
A program may use at most 64 MiB of HBM per device.

v0:
```python
import math

import jax
import jax.numpy as jnp
from jax import lax
from jax.sharding import PartitionSpec as P

SECTIONS = 4


EPSILON = 1e-05


def partner_2(value, axis, stride):
    mask = 2**stride
    pairs = [(source, source ^ mask) for source in range(lax.axis_size(axis))]
    return lax.ppermute(value, axis, pairs)


def gelu_back(preact, upstream):
    return jax.vjp(lambda value: jax.nn.gelu(value, approximate=False), preact)[1](upstream)[0]


def switch_forward(lower, upper, w_expand, b_expand):
    joined = jnp.concatenate([lower, upper], axis=-1).astype(jnp.float32)
    centred = joined - jnp.mean(joined, axis=-1, keepdims=True)
    inv_std = lax.rsqrt(jnp.mean(centred * centred, axis=-1, keepdims=True) + EPSILON)
    normed = centred * inv_std
    normed_low = normed.astype(jnp.bfloat16)
    preact = jnp.dot(normed_low, w_expand, preferred_element_type=jnp.float32) + b_expand
    hidden = jax.nn.gelu(preact, approximate=False).astype(jnp.bfloat16)
    return (joined, normed, inv_std, normed_low, preact, hidden)


def switch_apply(lower, upper, w_expand, b_expand, w_reduce, b_reduce, gate_logit):
    joined, normed, inv_std, normed_low, preact, hidden = switch_forward(
        lower, upper, w_expand, b_expand
    )
    mixed = jnp.dot(hidden, w_reduce, preferred_element_type=jnp.float32)
    result = (jax.nn.sigmoid(gate_logit) * joined + mixed + b_reduce).astype(jnp.bfloat16)
    width = lower.shape[-1]
    return (result[:, :width], result[:, width:])


def switch_backward(
    lower, upper, grad_lower, grad_upper, w_expand, b_expand, w_reduce, b_reduce, gate_logit
):
    joined, normed, inv_std, normed_low, preact, hidden = switch_forward(
        lower, upper, w_expand, b_expand
    )
    grad_out = jnp.concatenate([grad_lower, grad_upper], axis=-1)
    grad_float = grad_out.astype(jnp.float32)
    sigma = jax.nn.sigmoid(gate_logit)
    grad_bias_red = jnp.sum(grad_float, axis=0)
    grad_gate = jnp.sum(grad_float * joined, axis=0) * sigma * (1.0 - sigma)
    grad_weight_red = jnp.dot(hidden.T, grad_out, preferred_element_type=jnp.float32)
    grad_hidden = jnp.dot(grad_out, w_reduce.T, preferred_element_type=jnp.float32)
    grad_pre = gelu_back(preact, grad_hidden)
    grad_pre_low = grad_pre.astype(jnp.bfloat16)
    grad_bias_exp = jnp.sum(grad_pre, axis=0)
    grad_weight_exp = jnp.dot(normed_low.T, grad_pre_low, preferred_element_type=jnp.float32)
    grad_normed = jnp.dot(grad_pre_low, w_expand.T, preferred_element_type=jnp.float32)
    grad_joined = sigma * grad_float + inv_std * (
        grad_normed
        - jnp.mean(grad_normed, axis=-1, keepdims=True)
        - normed * jnp.mean(grad_normed * normed, axis=-1, keepdims=True)
    )
    grad_joined = grad_joined.astype(jnp.bfloat16)
    width = lower.shape[-1]
    return (
        grad_joined[:, :width],
        grad_joined[:, width:],
        (grad_weight_exp, grad_bias_exp, grad_weight_red, grad_bias_red, grad_gate),
    )


def body(inputs, w_expand, b_expand, w_reduce, b_reduce, gate_logit, cotangent):
    weights = (w_expand, b_expand, w_reduce, b_reduce, gate_logit)
    rows = inputs.shape[1]
    width = inputs.shape[2]
    devs = lax.axis_size("ctx")
    count = devs.bit_length() - 1
    position = lax.axis_index("ctx")
    totals = (
        jnp.zeros(w_expand.shape, jnp.float32),
        jnp.zeros(b_expand.shape, jnp.float32),
        jnp.zeros(w_reduce.shape, jnp.float32),
        jnp.zeros(b_reduce.shape, jnp.float32),
        jnp.zeros(gate_logit.shape, jnp.float32),
    )
    state = inputs.reshape(rows, width)
    saved = []
    for section in range(SECTIONS):
        bit = (count - 1 - section) % count
        upper_side = position >> bit & 1 == 1
        partner = partner_2(state, "ctx", bit)
        lower = jnp.where(upper_side, partner, state)
        upper = jnp.where(upper_side, state, partner)
        out_lower, out_upper = switch_apply(lower, upper, *weights)
        state = jnp.where(upper_side, out_upper, out_lower)
        saved.append((lower, upper, upper_side, bit))
    outputs = state.reshape(inputs.shape)
    grad_state = cotangent.reshape(rows, width)
    for section in reversed(range(SECTIONS)):
        lower, upper, upper_side, bit = saved[section]
        partner_grad = partner_2(grad_state, "ctx", bit)
        grad_lower = jnp.where(upper_side, partner_grad, grad_state)
        grad_upper = jnp.where(upper_side, grad_state, partner_grad)
        back_lower, back_upper, grads = switch_backward(
            lower, upper, grad_lower, grad_upper, *weights
        )
        grad_state = jnp.where(upper_side, back_upper, back_lower)
        totals = tuple((total + piece for total, piece in zip(totals, grads)))
    grad_inputs = grad_state.reshape(inputs.shape)
    share = 0.5
    factor = share / math.sqrt(lax.axis_size("rep") * devs * rows)
    part_expand, part_reduce = (
        lax.psum_scatter(totals[0], "ctx", scatter_dimension=0, tiled=True),
        lax.psum_scatter(totals[2], "ctx", scatter_dimension=0, tiled=True),
    )
    part_expand, part_reduce = (
        lax.psum(part_expand.astype(jnp.bfloat16), "rep").astype(jnp.float32),
        lax.psum(part_reduce.astype(jnp.bfloat16), "rep").astype(jnp.float32),
    )
    bias_expand, bias_reduce, gate_sum = lax.psum((totals[1], totals[3], totals[4]), ("ctx", "rep"))
    return (
        outputs,
        grad_inputs,
        part_expand * factor,
        bias_expand * factor,
        part_reduce * factor,
        bias_reduce * factor,
        gate_sum * factor,
    )


def solution(mesh):
    return jax.shard_map(
        body,
        mesh=mesh,
        in_specs=(P("rep", "ctx", None), P(), P(), P(), P(), P(), P("rep", "ctx", None)),
        out_specs=(
            P("rep", "ctx", None),
            P("rep", "ctx", None),
            P("ctx", None),
            P(),
            P("ctx", None),
            P(),
            P(),
        ),
        check_vma=False,
    )
```

profile of v0, /device:TPU:1, one launch (start us, length us, event | category | flops | bytes accessed | tf_op | source)
XLA Modules:
  0.0 865.5 jit_solution(2419286555103033543)
XLA Ops:
  7.2 3.9 collective-permute-start
  11.8 1.9 collective-permute-done
  13.7 0.9 broadcast_select_fusion.3
  15.0 4.6 multiply_convert_fusion.3
  20.1 5.0 collective-permute-start.1
  25.1 2.4 collective-permute-done.1
  27.9 3.8 multiply_convert_fusion.2
  31.6 0.8 copy-done.1
  32.9 3.0 collective-permute-start.2
  36.2 2.1 collective-permute-done.2
  38.7 2.6 multiply_convert_fusion.1
  41.8 1.6 collective-permute-start.3
  43.4 2.4 collective-permute-done.3
  46.3 2.6 multiply_convert_fusion
  50.3 1.2 fusion.48
  51.5 3.0 collective-permute-start.5
  55.1 1.9 collective-permute-done.5
  58.6 2.3 collective-permute-start.6
  61.5 1.8 collective-permute-done.6
  63.3 0.7 fusion.126
  65.0 3.4 collective-permute-start.7
  69.0 2.7 collective-permute-done.7
  72.5 2.0 add_add_fusion.1
  74.8 1.6 fusion.115
  77.9 1.8 add_add_fusion
  79.7 0.9 copy-done.6
  82.0 87.2 %all-reduce = (f32[1024]{0:T(1024)S(1)}, f32[512]{0:T(512)S(1)}, f32[512]{0:T(512)S(1)}) all-reduce(f32[1024]{0:T(1024)S(1)} %add_add_fusion.2, f32[512]{0:T(512)S(1)} %get-tuple-element.71, f32[512]{0:T(512)S(1)} %get-tuple-element.70), channel_id=1, replica_groups=mesh['ctx'=64,'rep'=4] {'ctx','rep'}, use_global_device_ids=true, to_apply=%region_22.23 | all-reduce | flops 2048 | bytes 16384 | tf_op jit(solution)/shard_map/psum | solution.py:125
  171.9 240.2 %reduce-scatter.3.cloned.1.call-done = f32[8,1024]{1,0:T(8,128)} async-done(((f32[512,1024]{1,0:T(8,128)}), f32[8,1024]{1,0:T(8,128)}) %reduce-scatter.3.cloned.1.call-update) | async-done | bytes 32784 | tf_op jit(solution)/shard_map/reduce_scatter | solution.py:118
  412.1 0.8 convert_element_type.136
  412.8 373.4 %reduce-scatter.5.cloned.1.call-done = f32[16,512]{1,0:T(8,128)} async-done(((f32[1024,512]{1,0:T(8,128)}), f32[16,512]{1,0:T(8,128)}) %reduce-scatter.5.cloned.1.call-update) | async-done | bytes 32784 | tf_op jit(solution)/shard_map/reduce_scatter | solution.py:119
  786.2 0.8 convert_element_type.138
  787.0 70.5 %all-reduce.1 = (bf16[8,1024]{1,0:T(8,128)(2,1)S(1)}, bf16[16,512]{1,0:T(8,128)(2,1)S(1)}) all-reduce(bf16[8,1024]{1,0:T(8,128)(2,1)S(1)} %convert_element_type.136, bf16[16,512]{1,0:T(8,128)(2,1)S(1)} %convert_element_type.138), channel_id=1, replica_groups=mesh['ctx'=64,'rep'=4] {'rep'}, use_global_device_ids=true, to_apply=%region_17.18 | all-reduce | flops 16384 | bytes 65536 | tf_op jit(solution)/shard_map/psum | solution.py:122
  (104 shorter events, 17.5 us)
Async XLA Ops:
  7.2 7.8 copy-start
  7.2 404.9 %reduce-scatter.3.cloned.1.call-start = ((), (), s32[]{:S(2)}) async-start(), calls=%async_computation.2 | async-start | bytes 2129920 | tf_op jit(solution)/shard_map/reduce_scatter | solution.py:118
  7.2 6.5 collective-permute-start
  15.0 4.6 copy-start.9
  15.0 4.6 copy-start.13
  19.6 8.3 copy-start.12
  20.1 7.4 collective-permute-start.1
  27.9 4.6 copy-start.10
  31.6 0.8 copy-start.1
  31.6 4.2 copy-start.7
  32.9 5.4 collective-permute-start.2
  35.9 7.5 collective-permute-start.4
  38.7 2.6 copy-start.11
  41.3 4.7 copy-start.3
  41.8 4.1 collective-permute-start.3
  48.9 1.4 copy-start.5
  51.5 5.4 collective-permute-start.5
  58.6 4.7 copy-start.16
  58.6 4.7 copy-start.17
  58.6 4.7 collective-permute-start.6
  65.0 6.8 copy-start.14
  65.0 6.8 copy-start.15
  65.0 6.7 collective-permute-start.7
  74.5 711.7 %reduce-scatter.5.cloned.1.call-start = ((), (), s32[]{:S(2)}) async-start(), calls=%async_computation.3 | async-start | bytes 2129920 | tf_op jit(solution)/shard_map/reduce_scatter | solution.py:119
  74.8 1.6 copy-start.4
  76.4 1.0 copy-start.2
  79.7 0.9 copy-start.6
  79.7 2.3 copy-start.8
Sparse Core Ops, SparseCore 0:
  74.6 337.3 reduce-scatter.2
  414.5 371.6 reduce-scatter.4
where the time goes:
time: 866 us
  waiting for transfers between devices  629 us (73%)
  blocking collectives  158 us (18%)
  matrix products  29.5 us (3%)
  starting transfers between devices  22.8 us (3%)
  between operations  14.5 us (2%)
  other arithmetic  9.87 us (1%)
    reduce_scatter x1, waiting for transfers between devices, body(): lax.psum_scatter(totals[2], 'ctx', scatter_dimension=0, tiled=True)  373 us
    reduce_scatter x1, waiting for transfers between devices, body(): lax.psum_scatter(totals[0], 'ctx', scatter_dimension=0, tiled=True)  240 us
    psum x1, blocking collectives, body(): lax.psum((totals[1], totals[3], totals[4]), ('ctx', 'rep'))  87.2 us
    psum x1, blocking collectives, body(): lax.psum(part_expand.astype(jnp.bfloat16), 'rep').astype(jnp.float32)  70.5 us
    ppermute x8, starting transfers between devices, partner_2(): return lax.ppermute(value, axis, pairs)  22.5 us
  transfers between devices with their start and end apart: 10, of which 9 were waited for; matrix products, arithmetic and copies ran while one was open for 2% of the time, Pallas kernels for 0%

commit v1 on v0

v1 whole, which is shorter than its diff:
```python
import functools
import math

import jax
import jax.numpy as jnp
from jax import lax
from jax.experimental import pallas as pl
from jax.experimental.pallas import tpu as pltpu
from jax.sharding import PartitionSpec as P

MESH = pl.DeviceIdType.MESH
F32 = jnp.float32
BF16 = jnp.bfloat16
EPSILON = 1e-05
SECTIONS = 4
GROUP = 16


def dot(a, b, dims):
    return lax.dot_general(a, b, (dims, ((), ())), preferred_element_type=F32)


NN = ((1,), (0,))
NT = ((1,), (1,))


def kernel(
    factor,
    x_ref,
    we_hbm,
    be_ref,
    wr_hbm,
    br_ref,
    gl_ref,
    ct_ref,
    out_ref,
    gin_ref,
    o_we,
    o_be,
    o_wr,
    o_br,
    o_gg,
    we,
    wr,
    st,
    gst,
    nrm,
    inv,
    norm_t,
    hid_t,
    dgelu,
    gout,
    gpre,
    own,
    sib,
    rsib,
    part,
    recv1,
    mid,
    recv2,
    zsend,
    zrecv,
    fin,
    rfin,
    acc_be,
    acc_br,
    acc_gg,
    vec,
    rvec,
    vx,
    vy,
    vz,
    load_sem,
    a_send,
    a_recv,
    c_send,
    c_recv,
    p_send,
    p_recv,
    q_send,
    q_recv,
    z_send,
    z_recv,
    b_send,
    b_recv,
):
    ctx = lax.axis_index("ctx")
    rep = lax.axis_index("rep")
    y = lax.rem(ctx, 4)
    member = lax.div(ctx, 4)
    x = lax.rem(member, 4)
    z_lo = lax.div(member, 4)
    core = lax.rem(rep, 2)
    z_hi = lax.div(rep, 2)
    z = z_hi * 4 + z_lo

    def at_member(m):
        return (m * 4 + y, rep)

    def at_x(v):
        return (z_lo * 16 + v * 4 + y, rep)

    def at_y(v):
        return (member * 4 + v, rep)

    def at_z(v):
        return (lax.rem(v, 4) * 16 + x * 4 + y, lax.div(v, 4) * 2 + core)

    sibling = (ctx, z_hi * 2 + 1 - core)

    def remote(src, dst, send, recv, device):
        return pltpu.make_async_remote_copy(
            src_ref=src, dst_ref=dst, send_sem=send, recv_sem=recv, device_id=device, device_id_type=MESH
        )

    load_we = pltpu.make_async_copy(we_hbm, we, load_sem.at[0])
    load_wr = pltpu.make_async_copy(wr_hbm, wr, load_sem.at[1])
    own_x = pltpu.make_async_copy(x_ref.at[member], st.at[0, member], load_sem.at[2])
    own_ct = pltpu.make_async_copy(ct_ref.at[member], gst.at[SECTIONS, member], load_sem.at[3])
    own_x.start()
    load_we.start()
    load_wr.start()
    own_ct.start()

    barrier = pltpu.get_barrier_semaphore()

    def hello(device):
        pl.semaphore_signal(barrier, inc=1, device_id=device, device_id_type=MESH)

    @pl.loop(1, GROUP)
    def _(o):
        hello(at_member(lax.rem(member + o, GROUP)))

    for o in range(1, 4):
        hello(at_y(lax.rem(y + o, 4)))
    for v in range(4):
        hello(at_z((1 - z_hi) * 4 + v))
    hello(sibling)
    pl.semaphore_wait(barrier, 23)

    def exchange(kind, src, dst):
        def copy(o):
            m = lax.rem(member + o, GROUP)
            return remote(src.at[m], dst.at[member], a_send.at[kind, o], a_recv.at[kind, o], at_member(m))

        def start():
            @pl.loop(1, GROUP)
            def _(o):
                copy(o).start()

        def arrive():
            @pl.loop(1, GROUP)
            def _(o):
                m = lax.rem(member + GROUP - o, GROUP)
                remote(src.at[m], dst.at[m], a_send.at[kind, o], a_recv.at[kind, o], at_member(m)).wait_recv()

        def sent():
            @pl.loop(1, GROUP)
            def _(o):
                copy(o).wait_send()

        return start, arrive, sent

    in_start, in_arrive, in_sent = exchange(0, x_ref, st.at[0])
    ct_start, ct_arrive, ct_sent = exchange(1, ct_ref, gst.at[SECTIONS])
    out_start, out_arrive, out_sent = exchange(2, st.at[SECTIONS], out_ref)
    gin_start, gin_arrive, gin_sent = exchange(3, gst.at[0], gin_ref)
    in_start()
    ct_start()

    acc_be[...] = jnp.zeros_like(acc_be)
    acc_br[...] = jnp.zeros_like(acc_br)
    acc_gg[...] = jnp.zeros_like(acc_gg)
    sigma = jax.nn.sigmoid(gl_ref[...])

    load_we.wait()
    load_wr.wait()
    own_x.wait()
    in_arrive()

    def joined_of(s):
        lower = st[s, 0:8].reshape(128, 256).astype(F32)
        upper = st[s, 8:16].reshape(128, 256).astype(F32)
        return jnp.concatenate([lower, upper], axis=1)

    def forward(s):
        cols = pl.ds(pl.multiple_of(s * 128, 128), 128)
        joined = joined_of(s)
        centred = joined - jnp.mean(joined, axis=1, keepdims=True)
        inv_std = lax.rsqrt(jnp.mean(centred * centred, axis=1, keepdims=True) + EPSILON)
        normed = centred * inv_std
        nrm[s] = normed
        inv[s] = inv_std
        low = normed.astype(BF16)
        norm_t[:, cols] = low.T
        mixed = sigma * joined + br_ref[...]
        for h in range(4):
            hs = slice(256 * h, 256 * h + 256)
            pre = dot(low, we[:, hs], NN) + be_ref[:, hs]
            cdf = 0.5 + 0.5 * lax.erf(pre * math.sqrt(0.5))
            pdf = jnp.exp(-0.5 * pre * pre) * (1.0 / math.sqrt(2.0 * math.pi))
            dgelu[s, :, hs] = cdf + pre * pdf
            hidden = (pre * cdf).astype(BF16)
            hid_t[hs, cols] = hidden.T
            mixed = mixed + dot(hidden, wr[hs, :], NN)
        result = mixed.astype(BF16)
        for j in range(8):
            st[s + 1, 2 * j] = result[16 * j : 16 * j + 16, :256]
            st[s + 1, 2 * j + 1] = result[16 * j : 16 * j + 16, 256:]

    @pl.loop(0, SECTIONS)
    def _(s):
        forward(s)

    out_start()
    own_out = pltpu.make_async_copy(st.at[SECTIONS, member], out_ref.at[member], load_sem.at[4])
    own_out.start()

    own_ct.wait()
    ct_arrive()

    def rows_of(s):
        return pl.ds(pl.multiple_of(s * 128, 128), 128)

    def upstream(s):
        lower = jnp.concatenate([gst[s + 1, 2 * j] for j in range(8)], axis=0)
        upper = jnp.concatenate([gst[s + 1, 2 * j + 1] for j in range(8)], axis=0)
        gout[rows_of(s), :] = jnp.concatenate([lower, upper], axis=1)

    def fold(v):
        return jnp.sum(v.reshape(16, 8, v.shape[1]), axis=0)

    def backward(s):
        grad = gout[rows_of(s), :]
        wide = grad.astype(F32)
        acc_br[...] += fold(wide)
        acc_gg[...] += fold(wide * joined_of(s))
        gnormed = None
        for h in range(4):
            hs = slice(256 * h, 256 * h + 256)
            pre = dot(grad, wr[hs, :], NT) * dgelu[s, :, hs]
            acc_be[:, hs] += fold(pre)
            low = pre.astype(BF16)
            gpre[rows_of(s), hs] = low
            term = dot(low, we[:, hs], NT)
            gnormed = term if gnormed is None else gnormed + term
        normed = nrm[s]
        mean = jnp.mean(gnormed, axis=1, keepdims=True)
        along = jnp.mean(gnormed * normed, axis=1, keepdims=True)
        result = (sigma * wide + inv[s] * (gnormed - mean - normed * along)).astype(BF16)
        gst[s, 0:8] = result[:, :256].reshape(8, 16, 256)
        gst[s, 8:16] = result[:, 256:].reshape(8, 16, 256)

    def core_copy(k):
        return remote(sib.at[k], rsib.at[k], c_send.at[k], c_recv.at[k], sibling)

    def gradient(k, mine):
        who = core if mine else 1 - core
        if k < 2:
            left = hid_t[512 * k : 512 * k + 512, :]
            right = gout[:, pl.ds(pl.multiple_of(256 * who, 256), 256)]
            blocks = dot(left, right, NN).reshape(2, 16, 16, 256)
        else:
            left = norm_t[...]
            right = gpre[:, pl.ds(pl.multiple_of(512 * who + 256 * (k - 2), 256), 256)]
            blocks = dot(left, right, NN).reshape(4, 16, 8, 256)
        value = jnp.concatenate([blocks[i] for i in range(blocks.shape[0])], axis=1)
        if mine:
            own[k] = value
        else:
            sib[k] = value.astype(BF16)

    def make(k):
        gradient(k, False)
        core_copy(k).start()
        gradient(k, True)

    x_first = (True, False, True, False)

    def first(k, o, to):
        if x_first[k]:
            v = lax.rem(x + o, 4)
            src = part.at[k, v]
            device = at_x(v)
        else:
            v = lax.rem(y + o, 4)
            src = part.at[k, :, v]
            device = at_y(v)
        return remote(src, recv1.at[k, o], p_send.at[k, o], p_recv.at[k, o], device)

    def second(k, o):
        if x_first[k]:
            v = lax.rem(y + o, 4)
            device = at_y(v)
        else:
            v = lax.rem(x + o, 4)
            device = at_x(v)
        return remote(mid.at[k, v], recv2.at[k, o], q_send.at[k, o], q_recv.at[k, o], device)

    def scatter(k):
        core_copy(k).wait_recv()
        total = own[k] + rsib[k].astype(F32)
        part[k] = total.astype(BF16).reshape(4, 4, 32, 256)
        for o in range(1, 4):
            first(k, o, True).start()

    def scatter_again(k):
        for o in range(1, 4):
            first(k, o, False).wait_recv()
        mine = part[k, x] if x_first[k] else part[k, :, y]
        total = mine.astype(F32)
        for o in range(1, 4):
            total = total + recv1[k, o].astype(F32)
        mid[k] = total.astype(BF16)
        for o in range(1, 4):
            second(k, o).start()

    def reduced(k):
        for o in range(1, 4):
            second(k, o).wait_recv()
        total = (mid[k, y] if x_first[k] else mid[k, x]).astype(F32)
        for o in range(1, 4):
            total = total + recv2[k, o].astype(F32)
        return total

    def z_copy(o):
        v = lax.rem(z + o, 8)
        return remote(zsend.at[lax.rem(v, 4)], zrecv.at[z], z_send.at[o], z_recv.at[o], at_z(v))

    def z_arrive(o):
        v = lax.rem(z + 8 - o, 8)
        remote(zsend.at[0], zrecv.at[v], z_send.at[o], z_recv.at[o], at_z(v)).wait_recv()

    def b_copy(n, o):
        sems = (b_send.at[n, o], b_recv.at[n, o])
        if n == 0:
            return remote(vec, rvec, *sems, sibling)
        if n == 1:
            return remote(vx.at[x], vx.at[x], *sems, at_x(lax.rem(x + o, 4)))
        if n == 2:
            return remote(vy.at[y], vy.at[y], *sems, at_y(lax.rem(y + o, 4)))
        return remote(vz.at[z], vz.at[z], *sems, at_z(lax.rem(z + o, 8)))

    def b_arrive(n, o):
        sems = (b_send.at[n, o], b_recv.at[n, o])
        if n == 0:
            remote(vec, rvec, *sems, sibling).wait_recv()
        elif n == 1:
            v = lax.rem(x + 4 - o, 4)
            remote(vx.at[v], vx.at[v], *sems, at_x(v)).wait_recv()
        elif n == 2:
            v = lax.rem(y + 4 - o, 4)
            remote(vy.at[v], vy.at[v], *sems, at_y(v)).wait_recv()
        else:
            v = lax.rem(z + 8 - o, 8)
            remote(vz.at[v], vz.at[v], *sems, at_z(v)).wait_recv()

    B_COUNT = (range(0, 1), range(1, 4), range(1, 4), range(1, 8))

    def b_begin(n):
        for o in B_COUNT[n]:
            b_copy(n, o).start()

    def b_end(n):
        for o in B_COUNT[n]:
            b_arrive(n, o)

    @pl.loop(0, SECTIONS - 1)
    def _(i):
        s = SECTIONS - 1 - i
        upstream(s)
        backward(s)

    upstream(0)
    make(0)
    make(1)
    scatter(0)
    backward(0)
    gin_start()
    own_gin = pltpu.make_async_copy(gst.at[0, member], gin_ref.at[member], load_sem.at[5])
    own_gin.start()
    scatter(1)
    make(2)
    make(3)

    def put(row, v):
        total = jnp.sum(v, axis=0, keepdims=True)
        for i in range(v.shape[1] // 256):
            vec[row + i : row + i + 1, :] = total[:, 256 * i : 256 * i + 256]

    put(0, acc_be[...])
    put(4, acc_br[...])
    put(6, acc_gg[...])
    b_begin(0)
    scatter(2)
    scatter_again(0)
    scatter(3)
    scatter_again(1)
    b_end(0)
    vx[x] = vec[...] + rvec[...]
    b_begin(1)
    f0 = reduced(0)
    f1 = reduced(1)
    for i in range(2):
        zsend[i, 0:16] = f0[16 * i : 16 * i + 16].astype(BF16)
        zsend[2 + i, 0:16] = f1[16 * i : 16 * i + 16].astype(BF16)
    scatter_again(2)
    scatter_again(3)
    b_end(1)
    vy[y] = (vx[0] + vx[1]) + (vx[2] + vx[3])
    b_begin(2)
    f2 = reduced(2)
    f3 = reduced(3)
    for i in range(4):
        rows = slice(8 * i, 8 * i + 8)
        zsend[i, 16:32] = jnp.concatenate([f2[rows], f3[rows]], axis=0).astype(BF16)
    for o in range(1, 8):
        z_copy(o).start()
    b_end(2)
    vz[z] = (vy[0] + vy[1]) + (vy[2] + vy[3])
    b_begin(3)
    zrecv[z] = zsend[z_lo]
    for o in range(1, 8):
        z_arrive(o)
    total = zrecv[0].astype(F32)
    for v in range(1, 8):
        total = total + zrecv[v].astype(F32)
    fin[...] = total * factor
    final = remote(fin, rfin, c_send.at[4], c_recv.at[4], sibling)
    final.start()
    b_end(3)
    small = vz[0]
    for v in range(1, 8):
        small = small + vz[v]
    small = small * factor
    for i in range(4):
        o_be[:, 256 * i : 256 * i + 256] = small[i : i + 1]
    for i in range(2):
        cols = slice(256 * i, 256 * i + 256)
        o_br[:, cols] = small[4 + i : 5 + i]
        sg = sigma[:, cols]
        o_gg[:, cols] = small[6 + i : 7 + i] * (sg * (1.0 - sg))

    def place(value, who):
        o_wr[:, pl.ds(pl.multiple_of(256 * who, 256), 256)] = value[0:16]
        for i in range(2):
            o_we[:, pl.ds(pl.multiple_of(512 * who + 256 * i, 256), 256)] = value[16 + 8 * i : 24 + 8 * i]

    place(fin[...], core)
    final.wait_recv()
    place(rfin[...], 1 - core)

    own_out.wait()
    own_gin.wait()
    out_arrive()
    gin_arrive()
    in_sent()
    ct_sent()
    out_sent()
    gin_sent()
    for k in range(4):
        core_copy(k).wait_send()
        for o in range(1, 4):
            first(k, o, True).wait_send()
            second(k, o).wait_send()
    final.wait_send()
    for o in range(1, 8):
        z_copy(o).wait_send()
    for n in range(4):
        for o in B_COUNT[n]:
            b_copy(n, o).wait_send()


def body(inputs, w_expand, b_expand, w_reduce, b_reduce, gate_logit, cotangent):
    rows, width = inputs.shape[1:]
    hidden = w_expand.shape[1]
    block = rows // GROUP
    factor = 1.0 / math.sqrt(lax.axis_size("rep") * lax.axis_size("ctx") * rows)
    any_spec = pl.BlockSpec(memory_space=pl.ANY)
    vmem = pl.BlockSpec(memory_space=pltpu.VMEM)
    dma = pltpu.SemaphoreType.DMA
    results = pl.pallas_call(
        functools.partial(kernel, factor),
        out_shape=(
            jax.ShapeDtypeStruct((GROUP, block, width), BF16),
            jax.ShapeDtypeStruct((GROUP, block, width), BF16),
            jax.ShapeDtypeStruct((8, 1024), F32),
            jax.ShapeDtypeStruct((1, 1024), F32),
            jax.ShapeDtypeStruct((16, 512), F32),
            jax.ShapeDtypeStruct((1, 512), F32),
            jax.ShapeDtypeStruct((1, 512), F32),
        ),
        in_specs=[any_spec, any_spec, vmem, any_spec, vmem, vmem, any_spec],
        out_specs=(any_spec, any_spec, vmem, vmem, vmem, vmem, vmem),
        scratch_shapes=[
            pltpu.VMEM((512, 1024), BF16),
            pltpu.VMEM((1024, 512), BF16),
            pltpu.VMEM((SECTIONS + 1, 16, 16, 256), BF16),
            pltpu.VMEM((SECTIONS + 1, 16, 16, 256), BF16),
            pltpu.VMEM((SECTIONS, 128, 512), F32),
            pltpu.VMEM((SECTIONS, 128, 1), F32),
            pltpu.VMEM((512, 512), BF16),
            pltpu.VMEM((1024, 512), BF16),
            pltpu.VMEM((SECTIONS, 128, 1024), F32),
            pltpu.VMEM((512, 512), BF16),
            pltpu.VMEM((512, 1024), BF16),
            pltpu.VMEM((4, 16, 32, 256), F32),
            pltpu.VMEM((4, 16, 32, 256), BF16),
            pltpu.VMEM((4, 16, 32, 256), BF16),
            pltpu.VMEM((4, 4, 4, 32, 256), BF16),
            pltpu.VMEM((4, 4, 4, 32, 256), BF16),
            pltpu.VMEM((4, 4, 32, 256), BF16),
            pltpu.VMEM((4, 4, 32, 256), BF16),
            pltpu.VMEM((4, 32, 256), BF16),
            pltpu.VMEM((8, 32, 256), BF16),
            pltpu.VMEM((32, 256), F32),
            pltpu.VMEM((32, 256), F32),
            pltpu.VMEM((8, 1024), F32),
            pltpu.VMEM((8, 512), F32),
            pltpu.VMEM((8, 512), F32),
            pltpu.VMEM((8, 256), F32),
            pltpu.VMEM((8, 256), F32),
            pltpu.VMEM((4, 8, 256), F32),
            pltpu.VMEM((4, 8, 256), F32),
            pltpu.VMEM((8, 8, 256), F32),
            dma((6,)),
            dma((4, 16)),
            dma((4, 16)),
            dma((5,)),
            dma((5,)),
            dma((4, 4)),
            dma((4, 4)),
            dma((4, 4)),
            dma((4, 4)),
            dma((8,)),
            dma((8,)),
            dma((4, 8)),
            dma((4, 8)),
        ],
        compiler_params=pltpu.CompilerParams(collective_id=0, has_side_effects=True),
    )(
        inputs.reshape(GROUP, block, width),
        w_expand,
        b_expand.reshape(1, hidden),
        w_reduce,
        b_reduce.reshape(1, 2 * width),
        gate_logit.reshape(1, 2 * width),
        cotangent.reshape(GROUP, block, width),
    )
    out, gin, g_we, g_be, g_wr, g_br, g_gg = results
    return (
        out.reshape(inputs.shape),
        gin.reshape(inputs.shape),
        g_we,
        g_be.reshape(hidden),
        g_wr,
        g_br.reshape(2 * width),
        g_gg.reshape(2 * width),
    )


def solution(mesh):
    return jax.shard_map(
        body,
        mesh=mesh,
        in_specs=(P("rep", "ctx", None), P(), P(), P(), P(), P(), P("rep", "ctx", None)),
        out_specs=(
            P("rep", "ctx", None),
            P("rep", "ctx", None),
            P("ctx", None),
            P(),
            P("ctx", None),
            P(),
            P(),
        ),
        check_vma=False,
    )
```

time: 866 us -> 61.5 us (0.07)
  waiting for transfers between devices: 629 us -> 0 us
  blocking collectives: 158 us -> 0 us
  Pallas kernels: 0 us -> 55 us
  matrix products: 29.5 us -> 0 us
  starting transfers between devices: 22.8 us -> 0 us
  between operations: 14.5 us -> 0.66 us
  other arithmetic: 9.87 us -> 0 us
    reduce_scatter x2 -> x0, waiting for transfers between devices: 614 us -> none  [the longest x1 373 us: body(): lax.psum_scatter(totals[2], 'ctx', scatter_dimension=0, tiled=True)]
    psum x2 -> x0, blocking collectives: 158 us -> none  [the longest x1 87.2 us: body(): lax.psum((totals[1], totals[3], totals[4]), ('ctx', 'rep'))]
    pallas_call x0 -> x1, Pallas kernels: none -> 55 us  [body(): pl.pallas_call(functools.partial(kernel, factor), out_shape=(jax.ShapeDty...]
    dot_general x24 -> x0, matrix products: 29.5 us -> none  [the longest x4 13.5 us: switch_forward(): jnp.dot(normed_low, w_expand, preferred_element_type=jnp.float32) + b_expand]
    ppermute x8 -> x0, starting transfers between devices: 22.5 us -> none  [partner_2(): return lax.ppermute(value, axis, pairs)]
    ppermute x8 -> x0, waiting for transfers between devices: 15.2 us -> none  [partner_2(): return lax.ppermute(value, axis, pairs)]
  transfers between devices with their start and end apart: 10 -> 0, of which waited for: 9 -> 0; matrix products, arithmetic and copies ran while one was open for 2% -> 0% of each run, Pallas kernels for 0% -> 0%
where the time goes in v1:
time: 61.5 us; the launch traced here: 61.2 us
  Pallas kernels  55 us (89%)
  local copies, waits for them, and re-layouts  5.57 us (9%)
  between operations  0.66 us (1%)
    pallas_call x1, Pallas kernels, body(): pl.pallas_call(functools.partial(kernel, factor), out_shape=(jax.ShapeDty...  55 us
    unnamed x19, local copies, waits for them, and re-layouts  5.57 us

profile of v1, /device:TPU:1, one launch (start us, length us, event | category | flops | bytes accessed | tf_op | source)
XLA Modules:
  0.0 61.2 jit_solution(2110498387977319842)
XLA Ops:
  0.6 55.0 %shard_map.126 = (bf16[16,16,256]{2,1,0:T(8,128)(2,1)}, bf16[16,16,256]{2,1,0:T(8,128)(2,1)}, f32[8,1024]{1,0:T(8,128)}, f32[1,1024]{1,0:T(1,128)}, f32[16,512]{...) custom-call(bf16[16,16,256]{2,1,0:T(8,128)(2,1)} %bitcast.10, bf16[512,1024]{1,0:T(8,128)(2,1)} %we_hbm.1, ...), custom_call_target="tpu_custom_call" | custom-call | tf_op jit(solution)/shard_map/pallas_call | solution.py:482
  55.6 0.0 copy-start
  55.6 1.6 %copy.21 = bf16[1,256,256]{2,1,0:T(8,128)(2,1)} copy(bf16[1,256,256]{2,1,0:T(8,128)(2,1)} %bitcast.13) | data formatting | bytes 262144
  57.2 0.0 copy-done
  57.2 0.0 copy-start.2
  57.2 0.7 %copy.22 = bf16[1,256,256]{2,1,0:T(8,128)(2,1)} copy(bf16[1,256,256]{2,1,0:T(8,128)(2,1)S(1)} %bitcast.12) | data formatting | bytes 262144
  57.9 0.1 copy-done.2
  58.0 0.0 copy-start.3
  58.0 0.0 copy-start.1
  58.0 0.6 %copy.23 = f32[8,1024]{1,0:T(8,128)} copy(f32[8,1024]{1,0:T(8,128)S(1)} %copy-done.2) | data formatting | bytes 65536
  58.6 0.1 copy-done.3
  58.7 0.6 copy.24
  59.3 0.0 copy-done.1
  59.3 0.0 copy-start.5
  59.3 0.6 %copy.25 = f32[16,512]{1,0:T(8,128)} copy(f32[16,512]{1,0:T(8,128)S(1)} %copy-done.1) | data formatting | bytes 65536
  59.9 0.1 copy-done.5
  59.9 0.0 copy-start.4
  59.9 0.6 copy.26
  60.5 0.1 copy-done.4
  60.6 0.6 copy.27
Async XLA Ops:
  55.6 1.6 %copy-start = (bf16[16,16,256]{2,1,0:T(8,128)(2,1)S(1)}, bf16[16,16,256]{2,1,0:T(8,128)(2,1)}, u32[]{:S(2)}) copy-start(bf16[16,16,256]{2,1,0:T(8,128)(2,1)} %get-tuple-element.15) | copy-start | bytes 393220
  57.2 0.8 %copy-start.2 = (f32[8,1024]{1,0:T(8,128)S(1)}, f32[8,1024]{1,0:T(8,128)}, u32[]{:S(2)}) copy-start(f32[8,1024]{1,0:T(8,128)} %get-tuple-element.30) | copy-start | bytes 98308
  58.0 0.7 %copy-start.3 = (f32[1,1024]{1,0:T(1,128)S(1)}, f32[1,1024]{1,0:T(1,128)}, u32[]{:S(2)}) copy-start(f32[1,1024]{1,0:T(1,128)} %get-tuple-element.17) | copy-start | bytes 12292
  58.0 1.3 %copy-start.1 = (f32[16,512]{1,0:T(8,128)S(1)}, f32[16,512]{1,0:T(8,128)}, u32[]{:S(2)}) copy-start(f32[16,512]{1,0:T(8,128)} %get-tuple-element.32) | copy-start | bytes 98308
  59.3 0.7 %copy-start.5 = (f32[1,512]{1,0:T(1,128)S(1)}, f32[1,512]{1,0:T(1,128)}, u32[]{:S(2)}) copy-start(f32[1,512]{1,0:T(1,128)} %get-tuple-element.19) | copy-start | bytes 6148
  59.9 0.7 %copy-start.4 = (f32[1,512]{1,0:T(1,128)S(1)}, f32[1,512]{1,0:T(1,128)}, u32[]{:S(2)}) copy-start(f32[1,512]{1,0:T(1,128)} %get-tuple-element.20) | copy-start | bytes 6148

commit v2 on v1

--- a/solution.py
+++ b/solution.py
@@ -28,10 +28,10 @@
     factor,
     x_ref,
     we_hbm,
-    be_ref,
+    be_hbm,
     wr_hbm,
-    br_ref,
-    gl_ref,
+    br_hbm,
+    gl_hbm,
     ct_ref,
     out_ref,
     gin_ref,
@@ -42,6 +42,9 @@
     o_gg,
     we,
     wr,
+    be_ref,
+    br_ref,
+    gl_ref,
     st,
     gst,
     nrm,
@@ -51,7 +54,6 @@
     dgelu,
     gout,
     gpre,
-    own,
     sib,
     rsib,
     part,
@@ -121,6 +123,12 @@
     load_we.start()
     load_wr.start()
     own_ct.start()
+    small_loads = [
+        pltpu.make_async_copy(a, b, load_sem.at[6 + i])
+        for i, (a, b) in enumerate(((be_hbm, be_ref), (br_hbm, br_ref), (gl_hbm, gl_ref)))
+    ]
+    for load in small_loads:
+        load.start()
 
     barrier = pltpu.get_barrier_semaphore()
 
@@ -171,6 +179,8 @@
     acc_be[...] = jnp.zeros_like(acc_be)
     acc_br[...] = jnp.zeros_like(acc_br)
     acc_gg[...] = jnp.zeros_like(acc_gg)
+    for load in small_loads:
+        load.wait()
     sigma = jax.nn.sigmoid(gl_ref[...])
 
     load_we.wait()
@@ -230,20 +240,20 @@
     def fold(v):
         return jnp.sum(v.reshape(16, 8, v.shape[1]), axis=0)
 
-    def backward(s):
+    def backward_hidden(s):
         grad = gout[rows_of(s), :]
         wide = grad.astype(F32)
         acc_br[...] += fold(wide)
         acc_gg[...] += fold(wide * joined_of(s))
-        gnormed = None
         for h in range(4):
             hs = slice(256 * h, 256 * h + 256)
             pre = dot(grad, wr[hs, :], NT) * dgelu[s, :, hs]
             acc_be[:, hs] += fold(pre)
-            low = pre.astype(BF16)
-            gpre[rows_of(s), hs] = low
-            term = dot(low, we[:, hs], NT)
-            gnormed = term if gnormed is None else gnormed + term
+            gpre[rows_of(s), hs] = pre.astype(BF16)
+
+    def backward_joined(s):
+        wide = gout[rows_of(s), :].astype(F32)
+        gnormed = dot(gpre[rows_of(s), :], we[...], NT)
         normed = nrm[s]
         mean = jnp.mean(gnormed, axis=1, keepdims=True)
         along = jnp.mean(gnormed * normed, axis=1, keepdims=True)
@@ -254,8 +264,7 @@
     def core_copy(k):
         return remote(sib.at[k], rsib.at[k], c_send.at[k], c_recv.at[k], sibling)
 
-    def gradient(k, mine):
-        who = core if mine else 1 - core
+    def gradient(k, who):
         if k < 2:
             left = hid_t[512 * k : 512 * k + 512, :]
             right = gout[:, pl.ds(pl.multiple_of(256 * who, 256), 256)]
@@ -264,20 +273,15 @@
             left = norm_t[...]
             right = gpre[:, pl.ds(pl.multiple_of(512 * who + 256 * (k - 2), 256), 256)]
             blocks = dot(left, right, NN).reshape(4, 16, 8, 256)
-        value = jnp.concatenate([blocks[i] for i in range(blocks.shape[0])], axis=1)
-        if mine:
-            own[k] = value
-        else:
-            sib[k] = value.astype(BF16)
-
-    def make(k):
-        gradient(k, False)
+        return jnp.concatenate([blocks[i] for i in range(blocks.shape[0])], axis=1)
+
+    def give(k):
+        sib[k] = gradient(k, 1 - core).astype(BF16)
         core_copy(k).start()
-        gradient(k, True)
 
     x_first = (True, False, True, False)
 
-    def first(k, o, to):
+    def first(k, o):
         if x_first[k]:
             v = lax.rem(x + o, 4)
             src = part.at[k, v]
@@ -298,15 +302,15 @@
         return remote(mid.at[k, v], recv2.at[k, o], q_send.at[k, o], q_recv.at[k, o], device)
 
     def scatter(k):
+        mine = gradient(k, core)
         core_copy(k).wait_recv()
-        total = own[k] + rsib[k].astype(F32)
-        part[k] = total.astype(BF16).reshape(4, 4, 32, 256)
+        part[k] = (mine + rsib[k].astype(F32)).astype(BF16).reshape(4, 4, 32, 256)
         for o in range(1, 4):
-            first(k, o, True).start()
+            first(k, o).start()
 
     def scatter_again(k):
         for o in range(1, 4):
-            first(k, o, False).wait_recv()
+            first(k, o).wait_recv()
         mine = part[k, x] if x_first[k] else part[k, :, y]
         total = mine.astype(F32)
         for o in range(1, 4):
@@ -323,13 +327,31 @@
             total = total + recv2[k, o].astype(F32)
         return total
 
-    def z_copy(o):
+    def z_copy(half, o):
         v = lax.rem(z + o, 8)
-        return remote(zsend.at[lax.rem(v, 4)], zrecv.at[z], z_send.at[o], z_recv.at[o], at_z(v))
-
-    def z_arrive(o):
-        v = lax.rem(z + 8 - o, 8)
-        remote(zsend.at[0], zrecv.at[v], z_send.at[o], z_recv.at[o], at_z(v)).wait_recv()
+        return remote(
+            zsend.at[half, lax.rem(v, 4)], zrecv.at[half, z], z_send.at[half, o], z_recv.at[half, o], at_z(v)
+        )
+
+    def z_begin(half):
+        for o in range(1, 8):
+            z_copy(half, o).start()
+        zrecv[half, z] = zsend[half, z_lo]
+
+    def final_copy(half):
+        return remote(fin.at[half], rfin.at[half], c_send.at[4 + half], c_recv.at[4 + half], sibling)
+
+    def z_end(half):
+        for o in range(1, 8):
+            v = lax.rem(z + 8 - o, 8)
+            remote(
+                zsend.at[half, 0], zrecv.at[half, v], z_send.at[half, o], z_recv.at[half, o], at_z(v)
+            ).wait_recv()
+        total = zrecv[half, 0].astype(F32)
+        for v in range(1, 8):
+            total = total + zrecv[half, v].astype(F32)
+        fin[half] = total * factor
+        final_copy(half).start()
 
     def b_copy(n, o):
         sems = (b_send.at[n, o], b_recv.at[n, o])
@@ -369,65 +391,58 @@
     def _(i):
         s = SECTIONS - 1 - i
         upstream(s)
-        backward(s)
-
-    upstream(0)
-    make(0)
-    make(1)
-    scatter(0)
-    backward(0)
-    gin_start()
-    own_gin = pltpu.make_async_copy(gst.at[0, member], gin_ref.at[member], load_sem.at[5])
-    own_gin.start()
-    scatter(1)
-    make(2)
-    make(3)
+        backward_hidden(s)
+        backward_joined(s)
 
     def put(row, v):
         total = jnp.sum(v, axis=0, keepdims=True)
         for i in range(v.shape[1] // 256):
             vec[row + i : row + i + 1, :] = total[:, 256 * i : 256 * i + 256]
 
+    upstream(0)
+    give(0)
+    give(1)
+    backward_hidden(0)
+    scatter(0)
+    scatter(1)
+    give(2)
+    give(3)
+    backward_joined(0)
     put(0, acc_be[...])
     put(4, acc_br[...])
     put(6, acc_gg[...])
+    scatter(2)
+    scatter(3)
     b_begin(0)
-    scatter(2)
+    gin_start()
+    own_gin = pltpu.make_async_copy(gst.at[0, member], gin_ref.at[member], load_sem.at[5])
+    own_gin.start()
     scatter_again(0)
-    scatter(3)
     scatter_again(1)
     b_end(0)
     vx[x] = vec[...] + rvec[...]
     b_begin(1)
-    f0 = reduced(0)
-    f1 = reduced(1)
-    for i in range(2):
-        zsend[i, 0:16] = f0[16 * i : 16 * i + 16].astype(BF16)
-        zsend[2 + i, 0:16] = f1[16 * i : 16 * i + 16].astype(BF16)
+    for k in range(2):
+        block = reduced(k)
+        for i in range(2):
+            zsend[0, 2 * k + i] = block[16 * i : 16 * i + 16].astype(BF16)
+    z_begin(0)
     scatter_again(2)
     scatter_again(3)
     b_end(1)
     vy[y] = (vx[0] + vx[1]) + (vx[2] + vx[3])
     b_begin(2)
-    f2 = reduced(2)
-    f3 = reduced(3)
+    left = reduced(2)
+    right = reduced(3)
     for i in range(4):
         rows = slice(8 * i, 8 * i + 8)
-        zsend[i, 16:32] = jnp.concatenate([f2[rows], f3[rows]], axis=0).astype(BF16)
-    for o in range(1, 8):
-        z_copy(o).start()
+        zsend[1, i] = jnp.concatenate([left[rows], right[rows]], axis=0).astype(BF16)
+    z_begin(1)
     b_end(2)
     vz[z] = (vy[0] + vy[1]) + (vy[2] + vy[3])
     b_begin(3)
-    zrecv[z] = zsend[z_lo]
-    for o in range(1, 8):
-        z_arrive(o)
-    total = zrecv[0].astype(F32)
-    for v in range(1, 8):
-        total = total + zrecv[v].astype(F32)
-    fin[...] = total * factor
-    final = remote(fin, rfin, c_send.at[4], c_recv.at[4], sibling)
-    final.start()
+    z_end(0)
+    z_end(1)
     b_end(3)
     small = vz[0]
     for v in range(1, 8):
@@ -441,14 +456,18 @@
         sg = sigma[:, cols]
         o_gg[:, cols] = small[6 + i : 7 + i] * (sg * (1.0 - sg))
 
-    def place(value, who):
-        o_wr[:, pl.ds(pl.multiple_of(256 * who, 256), 256)] = value[0:16]
-        for i in range(2):
-            o_we[:, pl.ds(pl.multiple_of(512 * who + 256 * i, 256), 256)] = value[16 + 8 * i : 24 + 8 * i]
-
-    place(fin[...], core)
-    final.wait_recv()
-    place(rfin[...], 1 - core)
+    def place(half, value, who):
+        if half == 0:
+            o_wr[:, pl.ds(pl.multiple_of(256 * who, 256), 256)] = value
+        else:
+            for i in range(2):
+                o_we[:, pl.ds(pl.multiple_of(512 * who + 256 * i, 256), 256)] = value[8 * i : 8 * i + 8]
+
+    for half in range(2):
+        place(half, fin[half], core)
+    for half in range(2):
+        final_copy(half).wait_recv()
+        place(half, rfin[half], 1 - core)
 
     own_out.wait()
     own_gin.wait()
@@ -461,14 +480,36 @@
     for k in range(4):
         core_copy(k).wait_send()
         for o in range(1, 4):
-            first(k, o, True).wait_send()
+            first(k, o).wait_send()
             second(k, o).wait_send()
-    final.wait_send()
-    for o in range(1, 8):
-        z_copy(o).wait_send()
+    for half in range(2):
+        final_copy(half).wait_send()
+        for o in range(1, 8):
+            z_copy(half, o).wait_send()
     for n in range(4):
         for o in B_COUNT[n]:
             b_copy(n, o).wait_send()
+
+
+def finish(*refs):
+    n = len(refs) // 2
+    copies = [pltpu.make_async_copy(refs[i], refs[n + i], refs[2 * n].at[i]) for i in range(n)]
+    for copy in copies:
+        copy.start()
+    for copy in copies:
+        copy.wait()
+
+
+def hand_on(arrays):
+    n = len(arrays)
+    return pl.pallas_call(
+        finish,
+        out_shape=tuple(jax.ShapeDtypeStruct(a.shape, a.dtype) for a in arrays),
+        in_specs=[pl.BlockSpec(memory_space=pl.ANY)] * n,
+        out_specs=(pl.BlockSpec(memory_space=pltpu.HBM),) * n,
+        scratch_shapes=[pltpu.SemaphoreType.DMA((n,))],
+        compiler_params=pltpu.CompilerParams(vmem_limit_bytes=1024 * 1024),
+    )(*arrays)
 
 
 def body(inputs, w_expand, b_expand, w_reduce, b_reduce, gate_logit, cotangent):
@@ -490,11 +531,14 @@
             jax.ShapeDtypeStruct((1, 512), F32),
             jax.ShapeDtypeStruct((1, 512), F32),
         ),
-        in_specs=[any_spec, any_spec, vmem, any_spec, vmem, vmem, any_spec],
+        in_specs=[pl.BlockSpec(memory_space=pltpu.HBM)] * 7,
         out_specs=(any_spec, any_spec, vmem, vmem, vmem, vmem, vmem),
         scratch_shapes=[
             pltpu.VMEM((512, 1024), BF16),
             pltpu.VMEM((1024, 512), BF16),
+            pltpu.VMEM((1, 1024), F32),
+            pltpu.VMEM((1, 512), F32),
+            pltpu.VMEM((1, 512), F32),
             pltpu.VMEM((SECTIONS + 1, 16, 16, 256), BF16),
             pltpu.VMEM((SECTIONS + 1, 16, 16, 256), BF16),
             pltpu.VMEM((SECTIONS, 128, 512), F32),
@@ -504,17 +548,16 @@
             pltpu.VMEM((SECTIONS, 128, 1024), F32),
             pltpu.VMEM((512, 512), BF16),
             pltpu.VMEM((512, 1024), BF16),
-            pltpu.VMEM((4, 16, 32, 256), F32),
             pltpu.VMEM((4, 16, 32, 256), BF16),
             pltpu.VMEM((4, 16, 32, 256), BF16),
             pltpu.VMEM((4, 4, 4, 32, 256), BF16),
             pltpu.VMEM((4, 4, 4, 32, 256), BF16),
             pltpu.VMEM((4, 4, 32, 256), BF16),
             pltpu.VMEM((4, 4, 32, 256), BF16),
-            pltpu.VMEM((4, 32, 256), BF16),
-            pltpu.VMEM((8, 32, 256), BF16),
-            pltpu.VMEM((32, 256), F32),
-            pltpu.VMEM((32, 256), F32),
+            pltpu.VMEM((2, 4, 16, 256), BF16),
+            pltpu.VMEM((2, 8, 16, 256), BF16),
+            pltpu.VMEM((2, 16, 256), F32),
+            pltpu.VMEM((2, 16, 256), F32),
             pltpu.VMEM((8, 1024), F32),
             pltpu.VMEM((8, 512), F32),
             pltpu.VMEM((8, 512), F32),
@@ -523,31 +566,36 @@
             pltpu.VMEM((4, 8, 256), F32),
             pltpu.VMEM((4, 8, 256), F32),
             pltpu.VMEM((8, 8, 256), F32),
-            dma((6,)),
+            dma((9,)),
             dma((4, 16)),
             dma((4, 16)),
-            dma((5,)),
-            dma((5,)),
+            dma((6,)),
+            dma((6,)),
             dma((4, 4)),
             dma((4, 4)),
             dma((4, 4)),
             dma((4, 4)),
-            dma((8,)),
-            dma((8,)),
+            dma((2, 8)),
+            dma((2, 8)),
             dma((4, 8)),
             dma((4, 8)),
         ],
-        compiler_params=pltpu.CompilerParams(collective_id=0, has_side_effects=True),
+        compiler_params=pltpu.CompilerParams(collective_id=0, has_side_effects=True, vmem_limit_bytes=24 * 1024 * 1024),
     )(
-        inputs.reshape(GROUP, block, width),
-        w_expand,
-        b_expand.reshape(1, hidden),
-        w_reduce,
-        b_reduce.reshape(1, 2 * width),
-        gate_logit.reshape(1, 2 * width),
-        cotangent.reshape(GROUP, block, width),
+        *(
+            pltpu.with_memory_space_constraint(value, pltpu.HBM)
+            for value in (
+                inputs.reshape(GROUP, block, width),
+                w_expand,
+                b_expand.reshape(1, hidden),
+                w_reduce,
+                b_reduce.reshape(1, 2 * width),
+                gate_logit.reshape(1, 2 * width),
+                cotangent.reshape(GROUP, block, width),
+            )
+        )
     )
-    out, gin, g_we, g_be, g_wr, g_br, g_gg = results
+    out, gin, g_we, g_be, g_wr, g_br, g_gg = hand_on(results)
     return (
         out.reshape(inputs.shape),
         gin.reshape(inputs.shape),

time: 61.5 us -> 51.4 us (0.84)
  local copies, waits for them, and re-layouts: 5.57 us -> 0 us
  Pallas kernels: 55 us -> 50.7 us
    unnamed x19 -> x0, local copies, waits for them, and re-layouts: 5.57 us -> none
    pallas_call x1, Pallas kernels: 55 us -> 49.9 us  [body(): pl.pallas_call(functools.partial(kernel, factor), out_shape=(jax.ShapeDty...]
    pallas_call x0 -> x1, Pallas kernels: none -> 0.78 us  [hand_on(): pl.pallas_call(finish, out_shape=tuple((jax.ShapeDtypeStruct(a.shape, a.d...]
where the time goes in v2:
time: 51.4 us; the launch traced here: 51.3 us
  Pallas kernels  50.7 us (99%)
  between operations  0.64 us (1%)
    pallas_call x1, Pallas kernels, body(): pl.pallas_call(functools.partial(kernel, factor), out_shape=(jax.ShapeDty...  49.9 us

profile of v2, /device:TPU:1, one launch (start us, length us, event | category | flops | bytes accessed | tf_op | source)
XLA Modules:
  0.0 51.3 jit_solution(1293702064344132710)
XLA Ops:
  0.6 49.9 %shard_map.126 = (bf16[16,16,256]{2,1,0:T(8,128)(2,1)S(1)}, bf16[16,16,256]{2,1,0:T(8,128)(2,1)S(1)}, f32[8,1024]{1,0:T(8,128)S(1)}, f32[1,1024]{1,0:T(1,128)S(1...) custom-call(bf16[16,16,256]{2,1,0:T(8,128)(2,1)} %bitcast.10, bf16[512,1024]{1,0:T(8,128)(2,1)} %we_hbm.1, ...), custom_call_target="tpu_custom_call" | custom-call | tf_op jit(solution)/shard_map/pallas_call | solution.py:523
  50.5 0.8 %shard_map.127 = (bf16[16,16,256]{2,1,0:T(8,128)(2,1)}, bf16[16,16,256]{2,1,0:T(8,128)(2,1)}, f32[8,1024]{1,0:T(8,128)}, f32[1,1024]{1,0:T(1,128)}, f32[16,512]{...) custom-call(bf16[16,16,256]{2,1,0:T(8,128)(2,1)S(1)} %get-tuple-element.21.refs_0_, ...), custom_call_target="tpu_custom_call" | custom-call | tf_op jit(solution)/shard_map/pallas_call | solution.py:505

commit v3 on v2

--- a/solution.py
+++ b/solution.py
@@ -60,8 +60,6 @@
     recv1,
     mid,
     recv2,
-    zsend,
-    zrecv,
     fin,
     rfin,
     acc_be,
@@ -72,6 +70,7 @@
     vx,
     vy,
     vz,
+    small,
     load_sem,
     a_send,
     a_recv,
@@ -81,8 +80,8 @@
     p_recv,
     q_send,
     q_recv,
-    z_send,
-    z_recv,
+    f_send,
+    f_recv,
     b_send,
     b_recv,
 ):
@@ -99,16 +98,21 @@
     def at_member(m):
         return (m * 4 + y, rep)
 
+    def at(px, py, pz, pc):
+        return (lax.rem(pz, 4) * 16 + px * 4 + py, lax.div(pz, 4) * 2 + pc)
+
     def at_x(v):
-        return (z_lo * 16 + v * 4 + y, rep)
+        return at(v, y, z, core)
 
     def at_y(v):
-        return (member * 4 + v, rep)
+        return at(x, v, z, core)
 
     def at_z(v):
-        return (lax.rem(v, 4) * 16 + x * 4 + y, lax.div(v, 4) * 2 + core)
+        return at(x, y, v, core)
 
     sibling = (ctx, z_hi * 2 + 1 - core)
+    across = (ctx, (1 - z_hi) * 2 + core)
+    opposite = (ctx, (1 - z_hi) * 2 + 1 - core)
 
     def remote(src, dst, send, recv, device):
         return pltpu.make_async_remote_copy(
@@ -135,16 +139,19 @@
     def hello(device):
         pl.semaphore_signal(barrier, inc=1, device_id=device, device_id_type=MESH)
 
-    @pl.loop(1, GROUP)
+    @pl.loop(1, 32)
     def _(o):
-        hello(at_member(lax.rem(member + o, GROUP)))
-
-    for o in range(1, 4):
-        hello(at_y(lax.rem(y + o, 4)))
-    for v in range(4):
-        hello(at_z((1 - z_hi) * 4 + v))
+        v = lax.rem(z + lax.rem(o, 8), 8)
+        hello(at(lax.rem(x + lax.div(o, 8), 4), y, v, core))
+
+    @pl.loop(0, 15)
+    def _(o):
+        v = lax.rem(z + 6 + lax.rem(o, 5), 8)
+        hello(at(x, lax.rem(y + 1 + lax.div(o, 5), 4), v, core))
+
     hello(sibling)
-    pl.semaphore_wait(barrier, 23)
+    hello(opposite)
+    pl.semaphore_wait(barrier, 48)
 
     def exchange(kind, src, dst):
         def copy(o):
@@ -264,19 +271,19 @@
     def core_copy(k):
         return remote(sib.at[k], rsib.at[k], c_send.at[k], c_recv.at[k], sibling)
 
-    def gradient(k, who):
-        if k < 2:
-            left = hid_t[512 * k : 512 * k + 512, :]
-            right = gout[:, pl.ds(pl.multiple_of(256 * who, 256), 256)]
-            blocks = dot(left, right, NN).reshape(2, 16, 16, 256)
-        else:
-            left = norm_t[...]
-            right = gpre[:, pl.ds(pl.multiple_of(512 * who + 256 * (k - 2), 256), 256)]
-            blocks = dot(left, right, NN).reshape(4, 16, 8, 256)
-        return jnp.concatenate([blocks[i] for i in range(blocks.shape[0])], axis=1)
-
-    def give(k):
-        sib[k] = gradient(k, 1 - core).astype(BF16)
+    def reduce_quarters(who):
+        right = gout[:, pl.ds(pl.multiple_of(256 * who, 256), 256)]
+        blocks = dot(hid_t[...], right, NN).reshape(4, 16, 16, 256)
+        return [[blocks[q, :, :, 128 * k : 128 * k + 128] for q in range(4)] for k in range(2)]
+
+    def expand_quarters(k, who):
+        right = gpre[:, pl.ds(pl.multiple_of(512 * who + 256 * (k - 2), 256), 256)]
+        blocks = dot(norm_t[...], right, NN).reshape(4, 16, 8, 256)
+        return [jnp.concatenate([blocks[q, :, :, :128], blocks[q, :, :, 128:]], axis=1) for q in range(4)]
+
+    def give(k, quarters):
+        for q in range(4):
+            sib[k, :, q] = quarters[q].astype(BF16)
         core_copy(k).start()
 
     x_first = (True, False, True, False)
@@ -292,92 +299,78 @@
             device = at_y(v)
         return remote(src, recv1.at[k, o], p_send.at[k, o], p_recv.at[k, o], device)
 
-    def second(k, o):
-        if x_first[k]:
-            v = lax.rem(y + o, 4)
-            device = at_y(v)
-        else:
-            v = lax.rem(x + o, 4)
-            device = at_x(v)
-        return remote(mid.at[k, v], recv2.at[k, o], q_send.at[k, o], q_recv.at[k, o], device)
-
-    def scatter(k):
-        mine = gradient(k, core)
+    def scatter(k, quarters):
         core_copy(k).wait_recv()
-        part[k] = (mine + rsib[k].astype(F32)).astype(BF16).reshape(4, 4, 32, 256)
+        for q in range(4):
+            total = quarters[q] + rsib[k, :, q].astype(F32)
+            part[k, :, :, q] = total.astype(BF16).reshape(4, 4, 16, 128)
         for o in range(1, 4):
             first(k, o).start()
+
+    def second(k, j):
+        dv, step = divmod(j, 4)
+        dz = (0, 1, 2 if x_first[k] else 6, 7)[step]
+        v = lax.rem((y if x_first[k] else x) + dv, 4)
+        pz = lax.rem(z + dz, 8)
+        device = at(x, v, pz, core) if x_first[k] else at(v, y, pz, core)
+        return remote(
+            mid.at[k, v, lax.rem(pz, 4)], recv2.at[k, j], q_send.at[k, j], q_recv.at[k, j], device
+        )
 
     def scatter_again(k):
         for o in range(1, 4):
             first(k, o).wait_recv()
-        mine = part[k, x] if x_first[k] else part[k, :, y]
-        total = mine.astype(F32)
+        total = (part[k, x] if x_first[k] else part[k, :, y]).astype(F32)
         for o in range(1, 4):
             total = total + recv1[k, o].astype(F32)
         mid[k] = total.astype(BF16)
-        for o in range(1, 4):
-            second(k, o).start()
-
-    def reduced(k):
-        for o in range(1, 4):
-            second(k, o).wait_recv()
-        total = (mid[k, y] if x_first[k] else mid[k, x]).astype(F32)
-        for o in range(1, 4):
-            total = total + recv2[k, o].astype(F32)
-        return total
-
-    def z_copy(half, o):
-        v = lax.rem(z + o, 8)
-        return remote(
-            zsend.at[half, lax.rem(v, 4)], zrecv.at[half, z], z_send.at[half, o], z_recv.at[half, o], at_z(v)
-        )
-
-    def z_begin(half):
-        for o in range(1, 8):
-            z_copy(half, o).start()
-        zrecv[half, z] = zsend[half, z_lo]
-
-    def final_copy(half):
-        return remote(fin.at[half], rfin.at[half], c_send.at[4 + half], c_recv.at[4 + half], sibling)
-
-    def z_end(half):
-        for o in range(1, 8):
-            v = lax.rem(z + 8 - o, 8)
-            remote(
-                zsend.at[half, 0], zrecv.at[half, v], z_send.at[half, o], z_recv.at[half, o], at_z(v)
-            ).wait_recv()
-        total = zrecv[half, 0].astype(F32)
-        for v in range(1, 8):
-            total = total + zrecv[half, v].astype(F32)
-        fin[half] = total * factor
-        final_copy(half).start()
+        for j in range(1, 16):
+            second(k, j).start()
+
+    def final_copy(half, n):
+        device = (sibling, across, opposite)[n]
+        return remote(fin.at[half], rfin.at[n, half], f_send.at[half, n], f_recv.at[half, n], device)
+
+    def reduced(half):
+        for k in (2 * half, 2 * half + 1):
+            for j in range(1, 16):
+                second(k, j).wait_recv()
+            total = mid[k, y if x_first[k] else x, z_lo].astype(F32)
+            for j in range(1, 16):
+                total = total + recv2[k, j].astype(F32)
+            fin[half, k - 2 * half] = total.astype(BF16)
+        for n in range(3):
+            final_copy(half, n).start()
 
     def b_copy(n, o):
         sems = (b_send.at[n, o], b_recv.at[n, o])
         if n == 0:
-            return remote(vec, rvec, *sems, sibling)
+            return remote(vec.at[1 - core], rvec, *sems, sibling)
         if n == 1:
             return remote(vx.at[x], vx.at[x], *sems, at_x(lax.rem(x + o, 4)))
         if n == 2:
             return remote(vy.at[y], vy.at[y], *sems, at_y(lax.rem(y + o, 4)))
-        return remote(vz.at[z], vz.at[z], *sems, at_z(lax.rem(z + o, 8)))
+        if n == 3:
+            return remote(vz.at[z], vz.at[z], *sems, at_z(lax.rem(z + o, 8)))
+        return remote(small.at[core], small.at[core], *sems, sibling)
 
     def b_arrive(n, o):
         sems = (b_send.at[n, o], b_recv.at[n, o])
         if n == 0:
-            remote(vec, rvec, *sems, sibling).wait_recv()
+            remote(vec.at[core], rvec, *sems, sibling).wait_recv()
         elif n == 1:
             v = lax.rem(x + 4 - o, 4)
             remote(vx.at[v], vx.at[v], *sems, at_x(v)).wait_recv()
         elif n == 2:
             v = lax.rem(y + 4 - o, 4)
             remote(vy.at[v], vy.at[v], *sems, at_y(v)).wait_recv()
-        else:
+        elif n == 3:
             v = lax.rem(z + 8 - o, 8)
             remote(vz.at[v], vz.at[v], *sems, at_z(v)).wait_recv()
-
-    B_COUNT = (range(0, 1), range(1, 4), range(1, 4), range(1, 8))
+        else:
+            remote(small.at[1 - core], small.at[1 - core], *sems, sibling).wait_recv()
+
+    B_COUNT = (range(0, 1), range(1, 4), range(1, 4), range(1, 8), range(0, 1))
 
     def b_begin(n):
         for o in B_COUNT[n]:
@@ -394,80 +387,73 @@
         backward_hidden(s)
         backward_joined(s)
 
-    def put(row, v):
+    def put(half, row, v):
         total = jnp.sum(v, axis=0, keepdims=True)
-        for i in range(v.shape[1] // 256):
-            vec[row + i : row + i + 1, :] = total[:, 256 * i : 256 * i + 256]
+        for i in range(v.shape[1] // 128):
+            vec[half, row + i : row + i + 1, :] = total[:, 128 * i : 128 * i + 128]
 
     upstream(0)
-    give(0)
-    give(1)
+    for k, quarters in enumerate(reduce_quarters(1 - core)):
+        give(k, quarters)
     backward_hidden(0)
-    scatter(0)
-    scatter(1)
-    give(2)
-    give(3)
+    for k, quarters in enumerate(reduce_quarters(core)):
+        scatter(k, quarters)
+    for k in (2, 3):
+        give(k, expand_quarters(k, 1 - core))
     backward_joined(0)
-    put(0, acc_be[...])
-    put(4, acc_br[...])
-    put(6, acc_gg[...])
-    scatter(2)
-    scatter(3)
+    put(0, 0, acc_be[...])
+    put(1, 0, acc_br[...])
+    put(1, 4, acc_gg[...])
     b_begin(0)
+    for k in (2, 3):
+        scatter(k, expand_quarters(k, core))
+    b_end(0)
+    vx[x] = vec[core] + rvec[...]
+    b_begin(1)
     gin_start()
     own_gin = pltpu.make_async_copy(gst.at[0, member], gin_ref.at[member], load_sem.at[5])
     own_gin.start()
     scatter_again(0)
     scatter_again(1)
-    b_end(0)
-    vx[x] = vec[...] + rvec[...]
-    b_begin(1)
-    for k in range(2):
-        block = reduced(k)
-        for i in range(2):
-            zsend[0, 2 * k + i] = block[16 * i : 16 * i + 16].astype(BF16)
-    z_begin(0)
-    scatter_again(2)
-    scatter_again(3)
     b_end(1)
     vy[y] = (vx[0] + vx[1]) + (vx[2] + vx[3])
     b_begin(2)
-    left = reduced(2)
-    right = reduced(3)
-    for i in range(4):
-        rows = slice(8 * i, 8 * i + 8)
-        zsend[1, i] = jnp.concatenate([left[rows], right[rows]], axis=0).astype(BF16)
-    z_begin(1)
+    scatter_again(2)
+    scatter_again(3)
     b_end(2)
     vz[z] = (vy[0] + vy[1]) + (vy[2] + vy[3])
     b_begin(3)
-    z_end(0)
-    z_end(1)
+    reduced(0)
+    reduced(1)
     b_end(3)
-    small = vz[0]
+    total = vz[0]
     for v in range(1, 8):
-        small = small + vz[v]
-    small = small * factor
+        total = total + vz[v]
+    small[core] = total * factor
+    b_begin(4)
+
+    def place(half, value, who):
+        for k in range(2):
+            if half == 0:
+                o_wr[:, pl.ds(pl.multiple_of(256 * who + 128 * k, 128), 128)] = value[k]
+            else:
+                for i in range(2):
+                    cols = pl.ds(pl.multiple_of(512 * who + 256 * k + 128 * i, 128), 128)
+                    o_we[:, cols] = value[k, 8 * i : 8 * i + 8]
+
+    for half in range(2):
+        for n in range(3):
+            final_copy(half, n).wait_recv()
+        place(half, (fin[half].astype(F32) + rfin[1, half].astype(F32)) * factor, core)
+        place(half, (rfin[0, half].astype(F32) + rfin[2, half].astype(F32)) * factor, 1 - core)
+    b_end(4)
+    for i in range(8):
+        o_be[:, 128 * i : 128 * i + 128] = small[0, i : i + 1]
     for i in range(4):
-        o_be[:, 256 * i : 256 * i + 256] = small[i : i + 1]
-    for i in range(2):
-        cols = slice(256 * i, 256 * i + 256)
-        o_br[:, cols] = small[4 + i : 5 + i]
+        cols = slice(128 * i, 128 * i + 128)
+        o_br[:, cols] = small[1, i : i + 1]
         sg = sigma[:, cols]
-        o_gg[:, cols] = small[6 + i : 7 + i] * (sg * (1.0 - sg))
-
-    def place(half, value, who):
-        if half == 0:
-            o_wr[:, pl.ds(pl.multiple_of(256 * who, 256), 256)] = value
-        else:
-            for i in range(2):
-                o_we[:, pl.ds(pl.multiple_of(512 * who + 256 * i, 256), 256)] = value[8 * i : 8 * i + 8]
-
-    for half in range(2):
-        place(half, fin[half], core)
-    for half in range(2):
-        final_copy(half).wait_recv()
-        place(half, rfin[half], 1 - core)
+        o_gg[:, cols] = small[1, 4 + i : 5 + i] * (sg * (1.0 - sg))
 
     own_out.wait()
     own_gin.wait()
@@ -481,12 +467,12 @@
         core_copy(k).wait_send()
         for o in range(1, 4):
             first(k, o).wait_send()
-            second(k, o).wait_send()
+        for j in range(1, 16):
+            second(k, j).wait_send()
     for half in range(2):
-        final_copy(half).wait_send()
-        for o in range(1, 8):
-            z_copy(half, o).wait_send()
-    for n in range(4):
+        for n in range(3):
+            final_copy(half, n).wait_send()
+    for n in range(5):
         for o in B_COUNT[n]:
             b_copy(n, o).wait_send()
 
@@ -548,37 +534,36 @@
             pltpu.VMEM((SECTIONS, 128, 1024), F32),
             pltpu.VMEM((512, 512), BF16),
             pltpu.VMEM((512, 1024), BF16),
-            pltpu.VMEM((4, 16, 32, 256), BF16),
-            pltpu.VMEM((4, 16, 32, 256), BF16),
-            pltpu.VMEM((4, 4, 4, 32, 256), BF16),
-            pltpu.VMEM((4, 4, 4, 32, 256), BF16),
-            pltpu.VMEM((4, 4, 32, 256), BF16),
-            pltpu.VMEM((4, 4, 32, 256), BF16),
-            pltpu.VMEM((2, 4, 16, 256), BF16),
-            pltpu.VMEM((2, 8, 16, 256), BF16),
-            pltpu.VMEM((2, 16, 256), F32),
-            pltpu.VMEM((2, 16, 256), F32),
+            pltpu.VMEM((4, 16, 4, 16, 128), BF16),
+            pltpu.VMEM((4, 16, 4, 16, 128), BF16),
+            pltpu.VMEM((4, 4, 4, 4, 16, 128), BF16),
+            pltpu.VMEM((4, 4, 4, 4, 16, 128), BF16),
+            pltpu.VMEM((4, 4, 4, 16, 128), BF16),
+            pltpu.VMEM((4, 16, 16, 128), BF16),
+            pltpu.VMEM((2, 2, 16, 128), BF16),
+            pltpu.VMEM((3, 2, 2, 16, 128), BF16),
             pltpu.VMEM((8, 1024), F32),
             pltpu.VMEM((8, 512), F32),
             pltpu.VMEM((8, 512), F32),
-            pltpu.VMEM((8, 256), F32),
-            pltpu.VMEM((8, 256), F32),
-            pltpu.VMEM((4, 8, 256), F32),
-            pltpu.VMEM((4, 8, 256), F32),
-            pltpu.VMEM((8, 8, 256), F32),
+            pltpu.VMEM((2, 8, 128), F32),
+            pltpu.VMEM((8, 128), F32),
+            pltpu.VMEM((4, 8, 128), F32),
+            pltpu.VMEM((4, 8, 128), F32),
+            pltpu.VMEM((8, 8, 128), F32),
+            pltpu.VMEM((2, 8, 128), F32),
             dma((9,)),
             dma((4, 16)),
             dma((4, 16)),
-            dma((6,)),
-            dma((6,)),
+            dma((4,)),
+            dma((4,)),
             dma((4, 4)),
             dma((4, 4)),
-            dma((4, 4)),
-            dma((4, 4)),
-            dma((2, 8)),
-            dma((2, 8)),
-            dma((4, 8)),
-            dma((4, 8)),
+            dma((4, 16)),
+            dma((4, 16)),
+            dma((2, 3)),
+            dma((2, 3)),
+            dma((5, 8)),
+            dma((5, 8)),
         ],
         compiler_params=pltpu.CompilerParams(collective_id=0, has_side_effects=True, vmem_limit_bytes=24 * 1024 * 1024),
     )(

time: 51.4 us -> 54.7 us (1.064)
  Pallas kernels: 50.7 us -> 53.9 us
    pallas_call x1, Pallas kernels: 49.9 us -> 53.1 us  [body(): pl.pallas_call(functools.partial(kernel, factor), out_shape=(jax.ShapeDty...]
where the time goes in v3:
time: 54.7 us; the launch traced here: 54.6 us
  Pallas kernels  53.9 us (99%)
  between operations  0.64 us (1%)
    pallas_call x1, Pallas kernels, body(): pl.pallas_call(functools.partial(kernel, factor), out_shape=(jax.ShapeDty...  53.1 us

profile of v3, /device:TPU:1, one launch (start us, length us, event | category | flops | bytes accessed | tf_op | source)
XLA Modules:
  0.0 54.6 jit_solution(4218129946265865974)
XLA Ops:
  0.6 53.1 %shard_map.126 = (bf16[16,16,256]{2,1,0:T(8,128)(2,1)S(1)}, bf16[16,16,256]{2,1,0:T(8,128)(2,1)S(1)}, f32[8,1024]{1,0:T(8,128)S(1)}, f32[1,1024]{1,0:T(1,128)S(1...) custom-call(bf16[16,16,256]{2,1,0:T(8,128)(2,1)} %bitcast.10, bf16[512,1024]{1,0:T(8,128)(2,1)} %we_hbm.1, ...), custom_call_target="tpu_custom_call" | custom-call | tf_op jit(solution)/shard_map/pallas_call | solution.py:509
  53.8 0.8 %shard_map.127 = (bf16[16,16,256]{2,1,0:T(8,128)(2,1)}, bf16[16,16,256]{2,1,0:T(8,128)(2,1)}, f32[8,1024]{1,0:T(8,128)}, f32[1,1024]{1,0:T(1,128)}, f32[16,512]{...) custom-call(bf16[16,16,256]{2,1,0:T(8,128)(2,1)S(1)} %get-tuple-element.21.refs_0_, ...), custom_call_target="tpu_custom_call" | custom-call | tf_op jit(solution)/shard_map/pallas_call | solution.py:491

commit v4 on v2

--- a/solution.py
+++ b/solution.py
@@ -54,8 +54,11 @@
     dgelu,
     gout,
     gpre,
-    sib,
-    rsib,
+    hid_s,
+    norm_s,
+    gout_s,
+    gpre_s,
+    own,
     part,
     recv1,
     mid,
@@ -72,11 +75,14 @@
     vx,
     vy,
     vz,
+    small,
     load_sem,
     a_send,
     a_recv,
     c_send,
     c_recv,
+    s_send,
+    s_recv,
     p_send,
     p_recv,
     q_send,
@@ -115,6 +121,20 @@
             src_ref=src, dst_ref=dst, send_sem=send, recv_sem=recv, device_id=device, device_id_type=MESH
         )
 
+    barrier = pltpu.get_barrier_semaphore()
+
+    def hello(device):
+        pl.semaphore_signal(barrier, inc=1, device_id=device, device_id_type=MESH)
+
+    @pl.loop(1, GROUP)
+    def _(o):
+        hello(at_member(lax.rem(member + o, GROUP)))
+
+    for o in range(1, 4):
+        hello(at_y(lax.rem(y + o, 4)))
+    for v in range(4):
+        hello(at_z((1 - z_hi) * 4 + v))
+    hello(sibling)
     load_we = pltpu.make_async_copy(we_hbm, we, load_sem.at[0])
     load_wr = pltpu.make_async_copy(wr_hbm, wr, load_sem.at[1])
     own_x = pltpu.make_async_copy(x_ref.at[member], st.at[0, member], load_sem.at[2])
@@ -130,20 +150,6 @@
     for load in small_loads:
         load.start()
 
-    barrier = pltpu.get_barrier_semaphore()
-
-    def hello(device):
-        pl.semaphore_signal(barrier, inc=1, device_id=device, device_id_type=MESH)
-
-    @pl.loop(1, GROUP)
-    def _(o):
-        hello(at_member(lax.rem(member + o, GROUP)))
-
-    for o in range(1, 4):
-        hello(at_y(lax.rem(y + o, 4)))
-    for v in range(4):
-        hello(at_z((1 - z_hi) * 4 + v))
-    hello(sibling)
     pl.semaphore_wait(barrier, 23)
 
     def exchange(kind, src, dst):
@@ -187,6 +193,27 @@
     load_wr.wait()
     own_x.wait()
     in_arrive()
+
+    def rows_of(s):
+        return pl.ds(pl.multiple_of(s * 128, 128), 128)
+
+    def share(kind, s):
+        rows = rows_of(s)
+        if kind == 0:
+            src, dst = hid_t.at[:, rows], hid_s.at[:, rows]
+        elif kind == 1:
+            src, dst = norm_t.at[:, rows], norm_s.at[:, rows]
+        elif kind == 2:
+            cols = pl.ds(pl.multiple_of(256 * (1 - core), 256), 256)
+            src, dst = gout.at[rows, cols], gout_s.at[rows]
+        else:
+            cols = pl.ds(pl.multiple_of(512 * (1 - core), 512), 512)
+            src, dst = gpre.at[rows, cols], gpre_s.at[rows]
+        return remote(src, dst, s_send.at[kind, s], s_recv.at[kind, s], sibling)
+
+    def shared(kind):
+        for s in range(SECTIONS):
+            share(kind, s).wait_recv()
 
     def joined_of(s):
         lower = st[s, 0:8].reshape(128, 256).astype(F32)
@@ -221,6 +248,8 @@
     @pl.loop(0, SECTIONS)
     def _(s):
         forward(s)
+        share(0, s).start()
+        share(1, s).start()
 
     out_start()
     own_out = pltpu.make_async_copy(st.at[SECTIONS, member], out_ref.at[member], load_sem.at[4])
@@ -228,9 +257,6 @@
 
     own_ct.wait()
     ct_arrive()
-
-    def rows_of(s):
-        return pl.ds(pl.multiple_of(s * 128, 128), 128)
 
     def upstream(s):
         lower = jnp.concatenate([gst[s + 1, 2 * j] for j in range(8)], axis=0)
@@ -261,23 +287,15 @@
         gst[s, 0:8] = result[:, :256].reshape(8, 16, 256)
         gst[s, 8:16] = result[:, 256:].reshape(8, 16, 256)
 
-    def core_copy(k):
-        return remote(sib.at[k], rsib.at[k], c_send.at[k], c_recv.at[k], sibling)
-
-    def gradient(k, who):
+    def product(k, hid, norm, grad, pre):
         if k < 2:
-            left = hid_t[512 * k : 512 * k + 512, :]
-            right = gout[:, pl.ds(pl.multiple_of(256 * who, 256), 256)]
-            blocks = dot(left, right, NN).reshape(2, 16, 16, 256)
-        else:
-            left = norm_t[...]
-            right = gpre[:, pl.ds(pl.multiple_of(512 * who + 256 * (k - 2), 256), 256)]
-            blocks = dot(left, right, NN).reshape(4, 16, 8, 256)
-        return jnp.concatenate([blocks[i] for i in range(blocks.shape[0])], axis=1)
-
-    def give(k):
-        sib[k] = gradient(k, 1 - core).astype(BF16)
-        core_copy(k).start()
+            return dot(hid[512 * k : 512 * k + 512, :], grad, NN)
+        return dot(norm[...], pre, NN)
+
+    def begin(k):
+        grad = gout[:, pl.ds(pl.multiple_of(256 * core, 256), 256)] if k < 2 else None
+        pre = gpre[:, pl.ds(pl.multiple_of(512 * core + 256 * (k - 2), 256), 256)] if k >= 2 else None
+        own[k] = product(k, hid_t, norm_t, grad, pre)
 
     x_first = (True, False, True, False)
 
@@ -302,9 +320,12 @@
         return remote(mid.at[k, v], recv2.at[k, o], q_send.at[k, o], q_recv.at[k, o], device)
 
     def scatter(k):
-        mine = gradient(k, core)
-        core_copy(k).wait_recv()
-        part[k] = (mine + rsib[k].astype(F32)).astype(BF16).reshape(4, 4, 32, 256)
+        grad = gout_s[...] if k < 2 else None
+        pre = gpre_s[:, 256 * (k - 2) : 256 * (k - 1)] if k >= 2 else None
+        total = own[k] + product(k, hid_s, norm_s, grad, pre)
+        blocks = total.reshape((2, 16, 16, 256) if k < 2 else (4, 16, 8, 256))
+        value = jnp.concatenate([blocks[i] for i in range(blocks.shape[0])], axis=1)
+        part[k] = value.astype(BF16).reshape(4, 4, 32, 256)
         for o in range(1, 4):
             first(k, o).start()
 
@@ -339,7 +360,7 @@
         zrecv[half, z] = zsend[half, z_lo]
 
     def final_copy(half):
-        return remote(fin.at[half], rfin.at[half], c_send.at[4 + half], c_recv.at[4 + half], sibling)
+        return remote(fin.at[half], rfin.at[half], c_send.at[half], c_recv.at[half], sibling)
 
     def z_end(half):
         for o in range(1, 8):
@@ -356,28 +377,32 @@
     def b_copy(n, o):
         sems = (b_send.at[n, o], b_recv.at[n, o])
         if n == 0:
-            return remote(vec, rvec, *sems, sibling)
+            return remote(vec.at[1 - core], rvec, *sems, sibling)
         if n == 1:
             return remote(vx.at[x], vx.at[x], *sems, at_x(lax.rem(x + o, 4)))
         if n == 2:
             return remote(vy.at[y], vy.at[y], *sems, at_y(lax.rem(y + o, 4)))
-        return remote(vz.at[z], vz.at[z], *sems, at_z(lax.rem(z + o, 8)))
+        if n == 3:
+            return remote(vz.at[z], vz.at[z], *sems, at_z(lax.rem(z + o, 8)))
+        return remote(small.at[core], small.at[core], *sems, sibling)
 
     def b_arrive(n, o):
         sems = (b_send.at[n, o], b_recv.at[n, o])
         if n == 0:
-            remote(vec, rvec, *sems, sibling).wait_recv()
+            remote(vec.at[core], rvec, *sems, sibling).wait_recv()
         elif n == 1:
             v = lax.rem(x + 4 - o, 4)
             remote(vx.at[v], vx.at[v], *sems, at_x(v)).wait_recv()
         elif n == 2:
             v = lax.rem(y + 4 - o, 4)
             remote(vy.at[v], vy.at[v], *sems, at_y(v)).wait_recv()
-        else:
+        elif n == 3:
             v = lax.rem(z + 8 - o, 8)
             remote(vz.at[v], vz.at[v], *sems, at_z(v)).wait_recv()
-
-    B_COUNT = (range(0, 1), range(1, 4), range(1, 4), range(1, 8))
+        else:
+            remote(small.at[1 - core], small.at[1 - core], *sems, sibling).wait_recv()
+
+    B_COUNT = (range(0, 1), range(1, 4), range(1, 4), range(1, 8), range(0, 1))
 
     def b_begin(n):
         for o in B_COUNT[n]:
@@ -391,70 +416,86 @@
     def _(i):
         s = SECTIONS - 1 - i
         upstream(s)
+        share(2, s).start()
         backward_hidden(s)
+        share(3, s).start()
         backward_joined(s)
 
-    def put(row, v):
+    def put(half, row, v):
         total = jnp.sum(v, axis=0, keepdims=True)
-        for i in range(v.shape[1] // 256):
-            vec[row + i : row + i + 1, :] = total[:, 256 * i : 256 * i + 256]
+        for i in range(v.shape[1] // 128):
+            vec[half, row + i : row + i + 1, :] = total[:, 128 * i : 128 * i + 128]
 
     upstream(0)
-    give(0)
-    give(1)
+    share(2, 0).start()
     backward_hidden(0)
+    share(3, 0).start()
+    begin(0)
+    begin(1)
+    put(0, 0, acc_be[...])
+    put(1, 0, acc_br[...])
+    put(1, 4, acc_gg[...])
+    b_begin(0)
+    shared(0)
+    shared(2)
     scatter(0)
     scatter(1)
-    give(2)
-    give(3)
-    backward_joined(0)
-    put(0, acc_be[...])
-    put(4, acc_br[...])
-    put(6, acc_gg[...])
+    begin(2)
+    begin(3)
+    b_end(0)
+    vx[x] = vec[core] + rvec[...]
+    b_begin(1)
+    shared(1)
+    shared(3)
     scatter(2)
     scatter(3)
-    b_begin(0)
+    backward_joined(0)
     gin_start()
     own_gin = pltpu.make_async_copy(gst.at[0, member], gin_ref.at[member], load_sem.at[5])
     own_gin.start()
+    in_sent()
+    ct_sent()
+    out_sent()
+    own_out.wait()
+    out_arrive()
     scatter_again(0)
     scatter_again(1)
-    b_end(0)
-    vx[x] = vec[...] + rvec[...]
-    b_begin(1)
+    b_end(1)
+    vy[y] = (vx[0] + vx[1]) + (vx[2] + vx[3])
+    b_begin(2)
+    scatter_again(2)
+    scatter_again(3)
     for k in range(2):
         block = reduced(k)
         for i in range(2):
             zsend[0, 2 * k + i] = block[16 * i : 16 * i + 16].astype(BF16)
     z_begin(0)
-    scatter_again(2)
-    scatter_again(3)
-    b_end(1)
-    vy[y] = (vx[0] + vx[1]) + (vx[2] + vx[3])
-    b_begin(2)
+    b_end(2)
+    vz[z] = (vy[0] + vy[1]) + (vy[2] + vy[3])
+    b_begin(3)
     left = reduced(2)
     right = reduced(3)
     for i in range(4):
         rows = slice(8 * i, 8 * i + 8)
         zsend[1, i] = jnp.concatenate([left[rows], right[rows]], axis=0).astype(BF16)
     z_begin(1)
-    b_end(2)
-    vz[z] = (vy[0] + vy[1]) + (vy[2] + vy[3])
-    b_begin(3)
     z_end(0)
+    b_end(3)
+    total = vz[0]
+    for v in range(1, 8):
+        total = total + vz[v]
+    small[core] = total * factor
+    b_begin(4)
+    own_gin.wait()
+    gin_arrive()
+    gin_sent()
+    for k in range(4):
+        for i in range(SECTIONS):
+            share(k, i).wait_send()
+        for o in range(1, 4):
+            first(k, o).wait_send()
+            second(k, o).wait_send()
     z_end(1)
-    b_end(3)
-    small = vz[0]
-    for v in range(1, 8):
-        small = small + vz[v]
-    small = small * factor
-    for i in range(4):
-        o_be[:, 256 * i : 256 * i + 256] = small[i : i + 1]
-    for i in range(2):
-        cols = slice(256 * i, 256 * i + 256)
-        o_br[:, cols] = small[4 + i : 5 + i]
-        sg = sigma[:, cols]
-        o_gg[:, cols] = small[6 + i : 7 + i] * (sg * (1.0 - sg))
 
     def place(half, value, who):
         if half == 0:
@@ -468,25 +509,20 @@
     for half in range(2):
         final_copy(half).wait_recv()
         place(half, rfin[half], 1 - core)
-
-    own_out.wait()
-    own_gin.wait()
-    out_arrive()
-    gin_arrive()
-    in_sent()
-    ct_sent()
-    out_sent()
-    gin_sent()
-    for k in range(4):
-        core_copy(k).wait_send()
-        for o in range(1, 4):
-            first(k, o).wait_send()
-            second(k, o).wait_send()
+    b_end(4)
+    for i in range(8):
+        o_be[:, 128 * i : 128 * i + 128] = small[0, i : i + 1]
+    for i in range(4):
+        cols = slice(128 * i, 128 * i + 128)
+        o_br[:, cols] = small[1, i : i + 1]
+        sg = sigma[:, cols]
+        o_gg[:, cols] = small[1, 4 + i : 5 + i] * (sg * (1.0 - sg))
+
     for half in range(2):
         final_copy(half).wait_send()
         for o in range(1, 8):
             z_copy(half, o).wait_send()
-    for n in range(4):
+    for n in range(5):
         for o in B_COUNT[n]:
             b_copy(n, o).wait_send()
 
@@ -548,8 +584,11 @@
             pltpu.VMEM((SECTIONS, 128, 1024), F32),
             pltpu.VMEM((512, 512), BF16),
             pltpu.VMEM((512, 1024), BF16),
-            pltpu.VMEM((4, 16, 32, 256), BF16),
-            pltpu.VMEM((4, 16, 32, 256), BF16),
+            pltpu.VMEM((1024, 512), BF16),
+            pltpu.VMEM((512, 512), BF16),
+            pltpu.VMEM((512, 256), BF16),
+            pltpu.VMEM((512, 512), BF16),
+            pltpu.VMEM((4, 512, 256), F32),
             pltpu.VMEM((4, 4, 4, 32, 256), BF16),
             pltpu.VMEM((4, 4, 4, 32, 256), BF16),
             pltpu.VMEM((4, 4, 32, 256), BF16),
@@ -561,24 +600,27 @@
             pltpu.VMEM((8, 1024), F32),
             pltpu.VMEM((8, 512), F32),
             pltpu.VMEM((8, 512), F32),
-            pltpu.VMEM((8, 256), F32),
-            pltpu.VMEM((8, 256), F32),
-            pltpu.VMEM((4, 8, 256), F32),
-            pltpu.VMEM((4, 8, 256), F32),
-            pltpu.VMEM((8, 8, 256), F32),
+            pltpu.VMEM((2, 8, 128), F32),
+            pltpu.VMEM((8, 128), F32),
+            pltpu.VMEM((4, 8, 128), F32),
+            pltpu.VMEM((4, 8, 128), F32),
+            pltpu.VMEM((8, 8, 128), F32),
+            pltpu.VMEM((2, 8, 128), F32),
             dma((9,)),
             dma((4, 16)),
             dma((4, 16)),
-            dma((6,)),
-            dma((6,)),
+            dma((2,)),
+            dma((2,)),
+            dma((4, SECTIONS)),
+            dma((4, SECTIONS)),
             dma((4, 4)),
             dma((4, 4)),
             dma((4, 4)),
             dma((4, 4)),
             dma((2, 8)),
             dma((2, 8)),
-            dma((4, 8)),
-            dma((4, 8)),
+            dma((5, 8)),
+            dma((5, 8)),
         ],
         compiler_params=pltpu.CompilerParams(collective_id=0, has_side_effects=True, vmem_limit_bytes=24 * 1024 * 1024),
     )(

time: 51.4 us -> 50.3 us (0.979)
  Pallas kernels: 50.7 us -> 49.6 us
    pallas_call x1, Pallas kernels: 49.9 us -> 48.8 us  [body(): pl.pallas_call(functools.partial(kernel, factor), out_shape=(jax.ShapeDty...]
where the time goes in v4:
time: 50.3 us; the launch traced here: 50.2 us
  Pallas kernels  49.6 us (99%)
  between operations  0.64 us (1%)
    pallas_call x1, Pallas kernels, body(): pl.pallas_call(functools.partial(kernel, factor), out_shape=(jax.ShapeDty...  48.8 us

profile of v4, /device:TPU:1, one launch (start us, length us, event | category | flops | bytes accessed | tf_op | source)
XLA Modules:
  0.0 50.2 jit_solution(7348841242384323656)
XLA Ops:
  0.6 48.8 %shard_map.126 = (bf16[16,16,256]{2,1,0:T(8,128)(2,1)S(1)}, bf16[16,16,256]{2,1,0:T(8,128)(2,1)S(1)}, f32[8,1024]{1,0:T(8,128)S(1)}, f32[1,1024]{1,0:T(1,128)S(1...) custom-call(bf16[16,16,256]{2,1,0:T(8,128)(2,1)} %bitcast.10, bf16[512,1024]{1,0:T(8,128)(2,1)} %we_hbm.1, ...), custom_call_target="tpu_custom_call" | custom-call | tf_op jit(solution)/shard_map/pallas_call | solution.py:559
  49.5 0.8 %shard_map.127 = (bf16[16,16,256]{2,1,0:T(8,128)(2,1)}, bf16[16,16,256]{2,1,0:T(8,128)(2,1)}, f32[8,1024]{1,0:T(8,128)}, f32[1,1024]{1,0:T(1,128)}, f32[16,512]{...) custom-call(bf16[16,16,256]{2,1,0:T(8,128)(2,1)S(1)} %get-tuple-element.21.refs_0_, ...), custom_call_target="tpu_custom_call" | custom-call | tf_op jit(solution)/shard_map/pallas_call | solution.py:541

commit v5 on v4

--- a/solution.py
+++ b/solution.py
@@ -326,7 +326,7 @@
         blocks = total.reshape((2, 16, 16, 256) if k < 2 else (4, 16, 8, 256))
         value = jnp.concatenate([blocks[i] for i in range(blocks.shape[0])], axis=1)
         part[k] = value.astype(BF16).reshape(4, 4, 32, 256)
-        for o in range(1, 4):
+        for o in (2, 1, 3):
             first(k, o).start()
 
     def scatter_again(k):
@@ -337,7 +337,7 @@
         for o in range(1, 4):
             total = total + recv1[k, o].astype(F32)
         mid[k] = total.astype(BF16)
-        for o in range(1, 4):
+        for o in (2, 1, 3):
             second(k, o).start()
 
     def reduced(k):
@@ -355,7 +355,7 @@
         )
 
     def z_begin(half):
-        for o in range(1, 8):
+        for o in (4, 3, 5, 2, 6, 1, 7):
             z_copy(half, o).start()
         zrecv[half, z] = zsend[half, z_lo]
 
@@ -450,9 +450,6 @@
     scatter(2)
     scatter(3)
     backward_joined(0)
-    gin_start()
-    own_gin = pltpu.make_async_copy(gst.at[0, member], gin_ref.at[member], load_sem.at[5])
-    own_gin.start()
     in_sent()
     ct_sent()
     out_sent()
@@ -465,6 +462,9 @@
     b_begin(2)
     scatter_again(2)
     scatter_again(3)
+    gin_start()
+    own_gin = pltpu.make_async_copy(gst.at[0, member], gin_ref.at[member], load_sem.at[5])
+    own_gin.start()
     for k in range(2):
         block = reduced(k)
         for i in range(2):

time: 50.3 us -> 49.4 us (0.982)
  Pallas kernels: 49.6 us -> 48.7 us
    pallas_call x1, Pallas kernels: 48.8 us -> 47.9 us  [body(): pl.pallas_call(functools.partial(kernel, factor), out_shape=(jax.ShapeDty...]
where the time goes in v5:
time: 49.4 us
  Pallas kernels  48.7 us (99%)
  between operations  0.64 us (1%)
    pallas_call x1, Pallas kernels, body(): pl.pallas_call(functools.partial(kernel, factor), out_shape=(jax.ShapeDty...  47.9 us

profile of v5, /device:TPU:1, one launch (start us, length us, event | category | flops | bytes accessed | tf_op | source)
XLA Modules:
  0.0 49.4 jit_solution(16698077257805963399)
XLA Ops:
  0.6 47.9 %shard_map.126 = (bf16[16,16,256]{2,1,0:T(8,128)(2,1)S(1)}, bf16[16,16,256]{2,1,0:T(8,128)(2,1)S(1)}, f32[8,1024]{1,0:T(8,128)S(1)}, f32[1,1024]{1,0:T(1,128)S(1...) custom-call(bf16[16,16,256]{2,1,0:T(8,128)(2,1)} %bitcast.10, bf16[512,1024]{1,0:T(8,128)(2,1)} %we_hbm.1, ...), custom_call_target="tpu_custom_call" | custom-call | tf_op jit(solution)/shard_map/pallas_call | solution.py:559
  48.6 0.8 %shard_map.127 = (bf16[16,16,256]{2,1,0:T(8,128)(2,1)}, bf16[16,16,256]{2,1,0:T(8,128)(2,1)}, f32[8,1024]{1,0:T(8,128)}, f32[1,1024]{1,0:T(1,128)}, f32[16,512]{...) custom-call(bf16[16,16,256]{2,1,0:T(8,128)(2,1)S(1)} %get-tuple-element.21.refs_0_, ...), custom_call_target="tpu_custom_call" | custom-call | tf_op jit(solution)/shard_map/pallas_call | solution.py:541

commit v6 on v5

--- a/solution.py
+++ b/solution.py
@@ -292,10 +292,13 @@
             return dot(hid[512 * k : 512 * k + 512, :], grad, NN)
         return dot(norm[...], pre, NN)
 
-    def begin(k):
+    def mine(k):
         grad = gout[:, pl.ds(pl.multiple_of(256 * core, 256), 256)] if k < 2 else None
         pre = gpre[:, pl.ds(pl.multiple_of(512 * core + 256 * (k - 2), 256), 256)] if k >= 2 else None
-        own[k] = product(k, hid_t, norm_t, grad, pre)
+        return product(k, hid_t, norm_t, grad, pre)
+
+    def begin(k):
+        own[k] = mine(k)
 
     x_first = (True, False, True, False)
 
@@ -322,7 +325,7 @@
     def scatter(k):
         grad = gout_s[...] if k < 2 else None
         pre = gpre_s[:, 256 * (k - 2) : 256 * (k - 1)] if k >= 2 else None
-        total = own[k] + product(k, hid_s, norm_s, grad, pre)
+        total = (own[k] if k < 2 else mine(k)) + product(k, hid_s, norm_s, grad, pre)
         blocks = total.reshape((2, 16, 16, 256) if k < 2 else (4, 16, 8, 256))
         value = jnp.concatenate([blocks[i] for i in range(blocks.shape[0])], axis=1)
         part[k] = value.astype(BF16).reshape(4, 4, 32, 256)
@@ -440,8 +443,6 @@
     shared(2)
     scatter(0)
     scatter(1)
-    begin(2)
-    begin(3)
     b_end(0)
     vx[x] = vec[core] + rvec[...]
     b_begin(1)
@@ -588,7 +589,7 @@
             pltpu.VMEM((512, 512), BF16),
             pltpu.VMEM((512, 256), BF16),
             pltpu.VMEM((512, 512), BF16),
-            pltpu.VMEM((4, 512, 256), F32),
+            pltpu.VMEM((2, 512, 256), F32),
             pltpu.VMEM((4, 4, 4, 32, 256), BF16),
             pltpu.VMEM((4, 4, 4, 32, 256), BF16),
             pltpu.VMEM((4, 4, 32, 256), BF16),

time: 49.4 us -> 49.4 us (level)
  no operation moved by 1% of the time
where the time goes in v6:
time: 49.4 us
  Pallas kernels  48.7 us (99%)
  between operations  0.64 us (1%)
    pallas_call x1, Pallas kernels, body(): pl.pallas_call(functools.partial(kernel, factor), out_shape=(jax.ShapeDty...  47.9 us

profile of v6, /device:TPU:1, one launch (start us, length us, event | category | flops | bytes accessed | tf_op | source)
XLA Modules:
  0.0 49.4 jit_solution(808903741120722354)
XLA Ops:
  0.6 47.9 %shard_map.126 = (bf16[16,16,256]{2,1,0:T(8,128)(2,1)S(1)}, bf16[16,16,256]{2,1,0:T(8,128)(2,1)S(1)}, f32[8,1024]{1,0:T(8,128)S(1)}, f32[1,1024]{1,0:T(1,128)S(1...) custom-call(bf16[16,16,256]{2,1,0:T(8,128)(2,1)} %bitcast.10, bf16[512,1024]{1,0:T(8,128)(2,1)} %we_hbm.1, ...), custom_call_target="tpu_custom_call" | custom-call | tf_op jit(solution)/shard_map/pallas_call | solution.py:560
  48.6 0.8 %shard_map.127 = (bf16[16,16,256]{2,1,0:T(8,128)(2,1)}, bf16[16,16,256]{2,1,0:T(8,128)(2,1)}, f32[8,1024]{1,0:T(8,128)}, f32[1,1024]{1,0:T(1,128)}, f32[16,512]{...) custom-call(bf16[16,16,256]{2,1,0:T(8,128)(2,1)S(1)} %get-tuple-element.21.refs_0_, ...), custom_call_target="tpu_custom_call" | custom-call | tf_op jit(solution)/shard_map/pallas_call | solution.py:542
